TPU v7x, 32 devices: a whole 2x2x4 slice. The times are simulated.
32 devices in a mesh: seq: 8 (over z, y), tensor: 4 (over x, core).
Axes of the slice: x: 2, y: 2, z: 4, core: 2. Of those that a mesh axis runs over, the one named last changes fastest.
Arguments:
- block_input: float32 [8192, 1024], P(('seq', 'tensor')), may hold values from -6 to 6
- lengths: int32 [8], replicated, may hold values from 512 to 2048, as said below
- ln_gain: bfloat16 [2, 1024], P(None, ('seq', 'tensor')), may hold values from 0.25 to 1.75
- ln_bias: bfloat16 [2, 1024], P(None, ('seq', 'tensor')), may hold values from -1.5 to 1.5
- qkv_weight: bfloat16 [2, 1024, 3, 1024], P(None, 'seq', None, 'tensor'), may hold values from -0.1875 to 0.1875
- qkv_bias: bfloat16 [2, 3, 16, 64], P(None, None, 'tensor', 'seq'), may hold values from -2.5 to 2.5
- out_weight: bfloat16 [2, 1024, 1024], P(None, 'seq', 'tensor'), may hold values from -0.75 to 0.75
- up_weight: bfloat16 [2, 1024, 4096], P(None, 'seq', 'tensor'), may hold values from -0.1875 to 0.1875
- up_bias: bfloat16 [2, 16, 256], P(None, 'tensor', 'seq'), may hold values from -2.5 to 2.5
- down_weight: bfloat16 [2, 1024, 4096], P(None, 'seq', 'tensor'), may hold values from -0.09375 to 0.09375
- out_bias: bfloat16 [2, 1024], P(None, ('seq', 'tensor')), may hold values from -2.5 to 2.5
- out_grad: float32 [8192, 1024], P(('seq', 'tensor')), may hold values from -6 to 6
Outputs:
- block_output: float32 [8192, 1024], P(('seq', 'tensor'))
- input_grad: float32 [8192, 1024], P(('seq', 'tensor'))
- ln_gain_grad: float32 [2, 1024], P(None, ('seq', 'tensor'))
- ln_bias_grad: float32 [2, 1024], P(None, ('seq', 'tensor'))
- qkv_weight_grad: float32 [2, 1024, 3, 1024], P(None, 'seq', None, 'tensor')
- qkv_bias_grad: float32 [2, 3, 16, 64], P(None, None, 'tensor', 'seq')
- out_weight_grad: float32 [2, 1024, 1024], P(None, 'seq', 'tensor')
- up_weight_grad: float32 [2, 1024, 4096], P(None, 'seq', 'tensor')
- up_bias_grad: float32 [2, 16, 256], P(None, 'tensor', 'seq')
- down_weight_grad: float32 [2, 1024, 4096], P(None, 'seq', 'tensor')
- out_bias_grad: float32 [2, 1024], P(None, ('seq', 'tensor'))
Inputs may be any that keep to these rules, and one draw needn't show every extreme that they name: `lengths`: each length is 512, 1024 or 2048; half of them are 512, a quarter 2 * 512 and a quarter 4 * 512, so that they sum to 8192.
All inputs are finite; a program needn't handle non-finite values.
Results may differ from a plain program's by a relative error of at most 0.022.
Values may be sent and summed in bfloat16 or wider, within the bound.
No kernel may reach another device: no remote copies, remote signals or barrier semaphores. Data moves between devices by JAX's collectives and lax.ppermute only.
A program may use at most 256 MiB of HBM per device.

v0:
```python
import jax
import jax.numpy as jnp
from jax import lax
from jax.sharding import PartitionSpec as P

HEAD_DIM = 64
ROT = 16


EPSILON = 1e-05
MASKED = -1e30


def passed_along(block, axis, distance):
    devices = range(lax.axis_size(axis))
    route = [(i - distance, i) for i in devices if i - distance in devices]
    return lax.ppermute(block, axis, route)


def layer_norm(values, gain, shift):
    center = values - jnp.mean(values, axis=1, keepdims=True)
    scale_inv = lax.rsqrt(jnp.mean(center * center, axis=1, keepdims=True) + EPSILON)
    unit = center * scale_inv
    return (unit * gain + shift, unit, scale_inv)


def norm_back(grad, unit, scale_inv, gain):
    scaled = grad * gain
    return scale_inv * (
        scaled
        - jnp.mean(scaled, axis=1, keepdims=True)
        - unit * jnp.mean(scaled * unit, axis=1, keepdims=True)
    )


def rotary_tables(offsets):
    exponent = jnp.arange(0, ROT, 2).astype(jnp.float32) / ROT
    angles = offsets.astype(jnp.float32)[:, None] * (10000.0 ** (-exponent))[None, :]
    angles = jnp.concatenate([angles, angles], axis=1)
    return (jnp.cos(angles), jnp.sin(angles))


def rotate(values, cosine, sine):
    half = ROT // 2
    turned = values[..., :ROT]
    swapped = jnp.concatenate([-turned[..., half:], turned[..., :half]], axis=-1)
    rotated = turned * cosine[:, None, :] + swapped * sine[:, None, :]
    return jnp.concatenate([rotated, values[..., ROT:]], axis=-1)


def rotate_back(grad, cosine, sine):
    half = ROT // 2
    turned = grad[..., :ROT]
    sined = turned * sine[:, None, :]
    back = jnp.concatenate([sined[..., half:], -sined[..., :half]], axis=-1)
    return jnp.concatenate([turned * cosine[:, None, :] + back, grad[..., ROT:]], axis=-1)


def heads_first(values):
    return jnp.transpose(values, (1, 0, 2))


def contract_rows(left, right):
    return lax.dot_general(
        left, right, (((0,), (0,)), ((), ())), preferred_element_type=jnp.float32
    )


def contract_cols(left, right):
    return lax.dot_general(
        left, right, (((1,), (1,)), ((), ())), preferred_element_type=jnp.float32
    )


def local(
    block_input,
    lengths,
    ln_gain,
    ln_bias,
    qkv_weight,
    qkv_bias,
    out_weight,
    up_weight,
    up_bias,
    down_weight,
    out_bias,
    out_grad,
):
    tensor_count = lax.axis_size("tensor")
    local_rows = block_input.shape[0]
    group = local_rows * tensor_count
    width = block_input.shape[1]
    layers = qkv_weight.shape[0]
    block_rows = min(512, group)
    blocks = group // block_rows
    scale = HEAD_DIM ** (-0.5)
    first = lax.axis_index("seq") * group
    positions = first + jnp.arange(group, dtype=jnp.int32)
    ends = jnp.cumsum(lengths)
    starts_of = jnp.sum(jnp.where(ends[None, :] <= positions[:, None], lengths[None, :], 0), axis=1)
    cosine, sine = rotary_tables(positions - starts_of)
    key_positions = first - 2 * group + jnp.arange(3 * group, dtype=jnp.int32)
    visible = (key_positions[None, :] >= starts_of[:, None]) & (
        key_positions[None, :] <= positions[:, None]
    )

    def softmax_block(query_block, keys, index):
        raw = contract_cols(query_block, keys) * scale
        mask_block = lax.slice_in_dim(visible, index * block_rows, (index + 1) * block_rows, axis=0)
        return jax.nn.softmax(jnp.where(mask_block, raw, MASKED), axis=1)

    def head_forward(pack):
        query_head, key_head, value_head = pack
        outputs = []
        for index in range(blocks):
            query_block = lax.slice_in_dim(
                query_head, index * block_rows, (index + 1) * block_rows, axis=0
            )
            probs = softmax_block(query_block, key_head, index).astype(jnp.bfloat16)
            outputs.append(jnp.dot(probs, value_head, preferred_element_type=jnp.float32))
        return jnp.concatenate(outputs, axis=0)

    def head_backward(pack):
        query_head, key_head, value_head, grad_head = pack
        outputs = []
        query_grads = []
        key_grad = jnp.zeros(key_head.shape, jnp.float32)
        value_grad = jnp.zeros(value_head.shape, jnp.float32)
        for index in range(blocks):
            lower = index * block_rows
            upper = lower + block_rows
            query_block = lax.slice_in_dim(query_head, lower, upper, axis=0)
            grad_block = lax.slice_in_dim(grad_head, lower, upper, axis=0)
            probs = softmax_block(query_block, key_head, index)
            probs_low = probs.astype(jnp.bfloat16)
            outputs.append(jnp.dot(probs_low, value_head, preferred_element_type=jnp.float32))
            probs_grad = contract_cols(grad_block, value_head)
            delta = jnp.sum(probs * probs_grad, axis=1, keepdims=True)
            score_grad = (probs * (probs_grad - delta)).astype(jnp.bfloat16)
            query_grads.append(
                jnp.dot(score_grad, key_head, preferred_element_type=jnp.float32) * scale
            )
            key_grad = key_grad + contract_rows(score_grad, query_block) * scale
            value_grad = value_grad + contract_rows(probs_low, grad_block)
        return (
            jnp.concatenate(outputs, axis=0),
            jnp.concatenate(query_grads, axis=0),
            key_grad,
            value_grad,
        )

    def branches(values, weights, small):
        joint_weight, mix_weight, rise_weight, fall_weight, joint_bias, rise_bias = weights
        gain = small[0].astype(jnp.float32)
        shift = small[1].astype(jnp.float32)
        normed, unit, scale_inv = layer_norm(values, gain, shift)
        normed_rows = lax.all_gather(normed.astype(jnp.bfloat16), "tensor", axis=0, tiled=True)
        head_width = joint_weight.shape[2]
        heads_here = head_width // HEAD_DIM
        joint = jnp.dot(
            normed_rows,
            joint_weight.reshape(width, 3 * head_width),
            preferred_element_type=jnp.float32,
        )
        joint = (joint + joint_bias.reshape(3 * head_width).astype(jnp.float32)).reshape(
            group, 3, heads_here, HEAD_DIM
        )
        query = rotate(joint[:, 0], cosine, sine).astype(jnp.bfloat16)
        own = jnp.stack([rotate(joint[:, 1], cosine, sine), joint[:, 2]]).astype(jnp.bfloat16)
        pieces = []
        for back in (2, 1):
            pieces.append(passed_along(own, "seq", back))
        window = jnp.concatenate(pieces + [own], axis=1)
        rise = jnp.dot(
            normed_rows, rise_weight, preferred_element_type=jnp.float32
        ) + rise_bias.reshape(-1).astype(jnp.float32)
        hidden = jax.nn.gelu(rise, approximate=False).astype(jnp.bfloat16)
        return (normed_rows, unit, scale_inv, query, window, rise, hidden)

    kept_inputs = []
    kept_small = []
    current = block_input
    for layer in range(layers):
        weights = (
            lax.all_gather(qkv_weight[layer], "seq", axis=0, tiled=True),
            lax.all_gather(out_weight[layer], "seq", axis=0, tiled=True),
            lax.all_gather(up_weight[layer], "seq", axis=0, tiled=True),
            lax.all_gather(down_weight[layer], "seq", axis=0, tiled=True),
            lax.all_gather(qkv_bias[layer], "seq", axis=2, tiled=True),
            lax.all_gather(up_bias[layer], "seq", axis=1, tiled=True),
        )
        small = (
            lax.all_gather(ln_gain[layer], ("seq", "tensor"), axis=0, tiled=True),
            lax.all_gather(ln_bias[layer], ("seq", "tensor"), axis=0, tiled=True),
            lax.all_gather(out_bias[layer], ("seq", "tensor"), axis=0, tiled=True),
        )
        normed_rows, unit, scale_inv, query, window, rise, hidden = branches(
            current, weights, small
        )
        head_width = query.shape[1] * HEAD_DIM
        mixed = lax.map(
            head_forward, (heads_first(query), heads_first(window[0]), heads_first(window[1]))
        )
        mixed = heads_first(mixed).reshape(group, head_width).astype(jnp.bfloat16)
        partial_sum = contract_cols(mixed, weights[1]) + contract_cols(hidden, weights[3])
        branch = lax.psum_scatter(
            partial_sum.astype(jnp.bfloat16), "tensor", scatter_dimension=0, tiled=True
        ).astype(jnp.float32)
        kept_inputs.append(current)
        kept_small.append(small)
        current = current + branch + small[2].astype(jnp.float32)[None, :]
    gradient = out_grad
    collected = []
    for layer in reversed(range(layers)):
        weights = (
            lax.all_gather(qkv_weight[layer], "seq", axis=0, tiled=True),
            lax.all_gather(out_weight[layer], "seq", axis=0, tiled=True),
            lax.all_gather(up_weight[layer], "seq", axis=0, tiled=True),
            lax.all_gather(down_weight[layer], "seq", axis=0, tiled=True),
            lax.all_gather(qkv_bias[layer], "seq", axis=2, tiled=True),
            lax.all_gather(up_bias[layer], "seq", axis=1, tiled=True),
        )
        joint_weight, mix_weight, rise_weight, fall_weight, joint_bias, rise_bias = weights
        small = kept_small[layer]
        gain = small[0].astype(jnp.float32)
        normed_rows, unit, scale_inv, query, window, rise, hidden = branches(
            kept_inputs[layer], weights, small
        )
        heads_here = query.shape[1]
        head_width = heads_here * HEAD_DIM
        bias_grad = jnp.sum(gradient, axis=0)
        grad_rows = lax.all_gather(gradient.astype(jnp.bfloat16), "tensor", axis=0, tiled=True)
        fall_grad = contract_rows(grad_rows, hidden)
        hidden_grad = jnp.dot(grad_rows, fall_weight, preferred_element_type=jnp.float32)
        unused, gelu_back = jax.vjp(lambda values: jax.nn.gelu(values, approximate=False), rise)
        rise_grad = gelu_back(hidden_grad)[0].astype(jnp.bfloat16)
        rise_bias_grad = jnp.sum(rise_grad, axis=0, dtype=jnp.float32).reshape(
            rise_bias.shape[0], -1
        )
        rise_weight_grad = contract_rows(normed_rows, rise_grad)
        normed_part = contract_cols(rise_grad, rise_weight)
        mixed_grad = jnp.dot(grad_rows, mix_weight, preferred_element_type=jnp.float32)
        mixed_grad = mixed_grad.astype(jnp.bfloat16).reshape(group, heads_here, HEAD_DIM)
        mixed, query_grad, key_grad, value_grad = lax.map(
            head_backward,
            (
                heads_first(query),
                heads_first(window[0]),
                heads_first(window[1]),
                heads_first(mixed_grad),
            ),
        )
        mixed = heads_first(mixed).reshape(group, head_width).astype(jnp.bfloat16)
        mix_weight_grad = contract_rows(grad_rows, mixed)
        stacked = jnp.stack([heads_first(key_grad), heads_first(value_grad)])
        own_grad = lax.slice_in_dim(stacked, 2 * group, 3 * group, axis=1)
        for back in (1, 2):
            piece = lax.slice_in_dim(stacked, (2 - back) * group, (3 - back) * group, axis=1)
            own_grad = own_grad + passed_along(piece.astype(jnp.bfloat16), "seq", -back).astype(
                piece.dtype
            )
        joint_grad = jnp.stack(
            [
                rotate_back(heads_first(query_grad), cosine, sine),
                rotate_back(own_grad[0], cosine, sine),
                own_grad[1],
            ],
            axis=1,
        )
        joint_grad = joint_grad.astype(jnp.bfloat16).reshape(group, 3 * head_width)
        joint_bias_grad = jnp.sum(joint_grad, axis=0, dtype=jnp.float32).reshape(
            3, heads_here, HEAD_DIM
        )
        joint_weight_grad = contract_rows(normed_rows, joint_grad).reshape(width, 3, head_width)
        normed_part = normed_part + contract_cols(
            joint_grad, joint_weight.reshape(width, 3 * head_width)
        )
        normed_grad = lax.psum_scatter(
            normed_part.astype(jnp.bfloat16), "tensor", scatter_dimension=0, tiled=True
        ).astype(jnp.float32)
        gain_grad = jnp.sum(normed_grad * unit, axis=0)
        shift_grad = jnp.sum(normed_grad, axis=0)
        gradient = gradient + norm_back(normed_grad, unit, scale_inv, gain[None, :])
        owned = (
            lax.psum_scatter(
                joint_weight_grad.astype(jnp.bfloat16), "seq", scatter_dimension=0, tiled=True
            ).astype(jnp.float32),
            lax.psum_scatter(
                mix_weight_grad.astype(jnp.bfloat16), "seq", scatter_dimension=0, tiled=True
            ).astype(jnp.float32),
            lax.psum_scatter(
                rise_weight_grad.astype(jnp.bfloat16), "seq", scatter_dimension=0, tiled=True
            ).astype(jnp.float32),
            lax.psum_scatter(
                fall_grad.astype(jnp.bfloat16), "seq", scatter_dimension=0, tiled=True
            ).astype(jnp.float32),
            lax.psum_scatter(
                joint_bias_grad.astype(jnp.bfloat16), "seq", scatter_dimension=2, tiled=True
            ).astype(jnp.float32),
            lax.psum_scatter(
                rise_bias_grad.astype(jnp.bfloat16), "seq", scatter_dimension=1, tiled=True
            ).astype(jnp.float32),
        )
        owned_small = (
            lax.psum_scatter(gain_grad, ("seq", "tensor"), scatter_dimension=0, tiled=True),
            lax.psum_scatter(shift_grad, ("seq", "tensor"), scatter_dimension=0, tiled=True),
            lax.psum_scatter(bias_grad, ("seq", "tensor"), scatter_dimension=0, tiled=True),
        )
        collected.append(
            (
                owned_small[0],
                owned_small[1],
                owned[0],
                owned[4],
                owned[1],
                owned[2],
                owned[5],
                owned[3],
                owned_small[2],
            )
        )
    collected = collected[::-1]
    stacked_grads = [jnp.stack([entry[member] for entry in collected]) for member in range(9)]
    return (
        current,
        gradient,
        stacked_grads[0],
        stacked_grads[1],
        stacked_grads[2],
        stacked_grads[3],
        stacked_grads[4],
        stacked_grads[5],
        stacked_grads[6],
        stacked_grads[7],
        stacked_grads[8],
    )


def solution(mesh):
    in_specs = (
        P(("seq", "tensor"), None),
        P(),
        P(None, ("seq", "tensor")),
        P(None, ("seq", "tensor")),
        P(None, "seq", None, "tensor"),
        P(None, None, "tensor", "seq"),
        P(None, "seq", "tensor"),
        P(None, "seq", "tensor"),
        P(None, "tensor", "seq"),
        P(None, "seq", "tensor"),
        P(None, ("seq", "tensor")),
        P(("seq", "tensor"), None),
    )
    out_specs = (
        P(("seq", "tensor"), None),
        P(("seq", "tensor"), None),
        P(None, ("seq", "tensor")),
        P(None, ("seq", "tensor")),
        P(None, "seq", None, "tensor"),
        P(None, None, "tensor", "seq"),
        P(None, "seq", "tensor"),
        P(None, "seq", "tensor"),
        P(None, "tensor", "seq"),
        P(None, "seq", "tensor"),
        P(None, ("seq", "tensor")),
    )
    return jax.shard_map(local, mesh=mesh, in_specs=in_specs, out_specs=out_specs, check_vma=False)
```

profile of v0, /device:TPU:0, one launch (start us, length us, event | category | flops | bytes accessed | tf_op | source)
XLA Modules:
  0.0 1678.7 jit_solution(14785322300311545122)
XLA Ops:
  13.5 43.4 %all-reduce.15 = (bf16[1024]{0:T(1024)(128)(2,1)S(1)}, bf16[1024]{0:T(1024)(128)(2,1)S(1)}, bf16[1024]{0:T(1024)(128)(2,1)}, bf16[1024]{0:T(1024)(128)(2,1)}, bf...) all-reduce(bf16[1024]{0:T(1024)(128)(2,1)S(1)} %dynamic-update-slic, ...), channel_id=3, replica_groups=mesh['seq'=8,'tensor'=4] {'seq','tensor'}, use_global_device_ids=true, to_apply=%add.1 | all-reduce | flops 6144 | bytes 24576
  63.6 30.5 %all-gather.6 = bf16[1,4,256]{1,0,2:T(2,128)(2,1)S(1)} all-gather(bf16[1,4,32]{1,0,2:T(2,128)(2,1)S(1)} %copy.185), channel_id=8, replica_groups=mesh['seq'=8,'tensor'=4] {'seq'}, dimensions={2}, use_global_device_ids=true | all-gather | bytes 2304 | tf_op jit(solution)/shard_map/all_gather | solution.py:190
  100.0 31.1 %all-gather.3 = bf16[1,3,4,64]{2,1,0,3:T(4,128)(2,1)S(1)} all-gather(bf16[1,3,4,8]{2,1,0,3:T(4,128)(2,1)S(1)} %copy.184), channel_id=5, replica_groups=mesh['seq'=8,'tensor'=4] {'seq'}, dimensions={3}, use_global_device_ids=true | all-gather | bytes 1728 | tf_op jit(solution)/shard_map/all_gather | solution.py:189
  132.2 34.7 %all-gather.4 = bf16[1,1024,256]{2,1,0:T(8,128)(2,1)} all-gather(bf16[1,128,256]{2,1,0:T(8,128)(2,1)S(1)} %get-tuple-element.553), channel_id=6, replica_groups=mesh['seq'=8,'tensor'=4] {'seq'}, dimensions={1}, use_global_device_ids=true | all-gather | bytes 589824 | tf_op jit(solution)/shard_map/all_gather | solution.py:186
  212.6 48.4 %while.52 = (s32[]{:T(128)}, bf16[4,1024,64]{1,2,0:T(8,128)(2,1)}, pred[1024,3072]{1,0:T(32,128)(4,1)}, bf16[4,1024,64]{2,1,0:T(8,128)(2,1)}, bf16[4,3072,64]{2,...) while((s32[]{:T(128)}, bf16[4,1024,64]{1,2,0:T(8,128)(2,1)}, ...), condition=%wide.region_9.10_spmd, body=%wide.region_4.9_spmd.sunk | while | flops 830732288 | bytes 63593140 | solution.py:201
  271.1 48.5 %reduce-scatter.21.cloned.1.call-done = bf16[256,1024]{1,0:T(8,128)(2,1)} async-done(((bf16[1024,1024]{1,0:T(8,128)(2,1)}), bf16[256,1024]{1,0:T(8,128)(2,1)}) %reduce-scatter.21.cloned.1.call-update) | async-done | bytes 524304 | tf_op jit(solution)/shard_map/reduce_scatter | solution.py:206
  326.9 30.6 %all-gather.15 = bf16[1,4,256]{1,0,2:T(2,128)(2,1)S(1)} all-gather(bf16[1,4,32]{1,0,2:T(2,128)(2,1)S(1)} %copy.188), channel_id=17, replica_groups=mesh['seq'=8,'tensor'=4] {'seq'}, dimensions={2}, use_global_device_ids=true | all-gather | bytes 2304 | tf_op jit(solution)/shard_map/all_gather | solution.py:190
  357.7 30.9 %all-gather.12 = bf16[1,3,4,64]{2,1,0,3:T(4,128)(2,1)S(1)} all-gather(bf16[1,3,4,8]{2,1,0,3:T(4,128)(2,1)S(1)} %copy.187), channel_id=14, replica_groups=mesh['seq'=8,'tensor'=4] {'seq'}, dimensions={3}, use_global_device_ids=true | all-gather | bytes 1728 | tf_op jit(solution)/shard_map/all_gather | solution.py:189
  388.8 31.4 %all-gather.13 = bf16[1,1024,256]{2,1,0:T(8,128)(2,1)S(1)} all-gather(bf16[1,128,256]{2,1,0:T(8,128)(2,1)S(1)} %copy-done.42), channel_id=15, replica_groups=mesh['seq'=8,'tensor'=4] {'seq'}, dimensions={1}, use_global_device_ids=true | all-gather | bytes 589824 | tf_op jit(solution)/shard_map/all_gather | solution.py:186
  437.3 41.4 %all-gather.45.cloned.1.call-done = bf16[1,1024,1024]{2,1,0:T(8,128)(2,1)} async-done(((bf16[1,128,1024]{2,1,0:T(8,128)(2,1)}), bf16[1,1024,1024]{2,1,0:T(8,128)(2,1)}) %all-gather.45.cloned.1.call-update) | async-done | bytes 2097168 | tf_op jit(solution)/shard_map/all_gather | solution.py:187
  493.6 43.5 %all-gather.47.cloned.1.call-done = bf16[1,1024,1024]{2,1,0:T(8,128)(2,1)} async-done(((bf16[1,128,1024]{2,1,0:T(8,128)(2,1)}), bf16[1,1024,1024]{2,1,0:T(8,128)(2,1)}) %all-gather.47.cloned.1.call-update) | async-done | bytes 2097168 | tf_op jit(solution)/shard_map/all_gather | solution.py:188
  563.2 160.7 %while.54 = (s32[]{:T(128)}, bf16[4,1024,64]{1,2,0:T(8,128)(2,1)}, f32[4,1024,64]{1,2,0:T(8,128)}, f32[4,3072,64]{1,2,0:T(8,128)}, f32[4,3072,64]{1,2,0:T(8,128)...) while((s32[]{:T(128)}, bf16[4,1024,64]{1,2,0:T(8,128)(2,1)}, ...), condition=%wide.region_27.28_spmd, body=%wide.region_20.27_spmd.sunk | while | flops 2470376448 | bytes 173719824 | solution.py:244
  762.8 48.8 %while.53 = (s32[]{:T(128)}, bf16[4,1024,64]{1,2,0:T(8,128)(2,1)}, pred[1024,3072]{1,0:T(32,128)(4,1)}, bf16[4,1024,64]{2,1,0:T(8,128)(2,1)}, bf16[4,3072,64]{2,...) while((s32[]{:T(128)}, bf16[4,1024,64]{1,2,0:T(8,128)(2,1)}, ...), condition=%wide.region_18.19_spmd, body=%wide.region_13.18_spmd.sunk | while | flops 830732288 | bytes 63593140 | solution.py:201
  818.8 48.9 %reduce-scatter.23.cloned.1.call-done = bf16[256,1024]{1,0:T(8,128)(2,1)} async-done(((bf16[1024,1024]{1,0:T(8,128)(2,1)}), bf16[256,1024]{1,0:T(8,128)(2,1)}) %reduce-scatter.23.cloned.1.call-update) | async-done | bytes 524304 | tf_op jit(solution)/shard_map/reduce_scatter | solution.py:206
  920.3 159.7 %while.55 = (s32[]{:T(128)}, bf16[4,1024,64]{1,2,0:T(8,128)(2,1)}, f32[4,1024,64]{1,2,0:T(8,128)}, f32[4,3072,64]{1,2,0:T(8,128)}, f32[4,3072,64]{1,2,0:T(8,128)...) while((s32[]{:T(128)}, bf16[4,1024,64]{1,2,0:T(8,128)(2,1)}, ...), condition=%wide.region_38.39_spmd, body=%wide.region_31.38_spmd.sunk | while | flops 2470376448 | bytes 161136864 | solution.py:244
  1162.6 41.6 %all-reduce.16 = (bf16[3,4,64]{2,1,0:T(4,128)(2,1)S(1)}, bf16[3,4,64]{2,1,0:T(4,128)(2,1)S(1)}) all-reduce(bf16[3,4,64]{2,1,0:T(4,128)(2,1)S(1)} %copy-done.60, bf16[3,4,64]{2,1,0:T(4,128)(2,1)S(1)} %get-tuple-element.477), channel_id=31, replica_groups=mesh['seq'=8,'tensor'=4] {'seq'}, use_global_device_ids=true, to_apply=%region_55.56.clone | all-reduce | flops 1536 | bytes 6144
  1206.6 34.4 %reduce-scatter.31.cloned.1.call-done = bf16[128,3,256]{2,0,1:T(8,128)(2,1)} async-done(((bf16[1024,3,256]{2,0,1:T(8,128)(2,1)}), bf16[128,3,256]{2,0,1:T(8,128)(2,1)}) %reduce-scatter.31.cloned.1.call-update) | async-done | bytes 196624 | tf_op jit(solution)/shard_map/reduce_scatter | solution.py:285
  1241.0 68.4 %reduce-scatter.29.cloned.1.call-done = bf16[128,3,256]{2,0,1:T(8,128)(2,1)} async-done(((bf16[1024,3,256]{2,0,1:T(8,128)(2,1)}), bf16[128,3,256]{2,0,1:T(8,128)(2,1)}) %reduce-scatter.29.cloned.1.call-update) | async-done | bytes 196624 | tf_op jit(solution)/shard_map/reduce_scatter | solution.py:285
  1311.4 68.8 %reduce-scatter.39.cloned.1.call-done = bf16[128,1024]{1,0:T(8,128)(2,1)} async-done(((bf16[1024,1024]{1,0:T(8,128)(2,1)}), bf16[128,1024]{1,0:T(8,128)(2,1)}) %reduce-scatter.39.cloned.1.call-update) | async-done | bytes 262160 | tf_op jit(solution)/shard_map/reduce_scatter | solution.py:291
  1380.2 71.0 %reduce-scatter.37.cloned.1.call-done = bf16[128,1024]{1,0:T(8,128)(2,1)} async-done(((bf16[1024,1024]{1,0:T(8,128)(2,1)}), bf16[128,1024]{1,0:T(8,128)(2,1)}) %reduce-scatter.37.cloned.1.call-update) | async-done | bytes 262160 | tf_op jit(solution)/shard_map/reduce_scatter | solution.py:291
  1453.2 68.8 %reduce-scatter.43.cloned.1.call-done = bf16[128,1024]{1,0:T(8,128)(2,1)} async-done(((bf16[1024,1024]{1,0:T(8,128)(2,1)}), bf16[128,1024]{1,0:T(8,128)(2,1)}) %reduce-scatter.43.cloned.1.call-update) | async-done | bytes 262160 | tf_op jit(solution)/shard_map/reduce_scatter | solution.py:294
  1522.0 71.2 %reduce-scatter.41.cloned.1.call-done = bf16[128,1024]{1,0:T(8,128)(2,1)} async-done(((bf16[1024,1024]{1,0:T(8,128)(2,1)}), bf16[128,1024]{1,0:T(8,128)(2,1)}) %reduce-scatter.41.cloned.1.call-update) | async-done | bytes 262160 | tf_op jit(solution)/shard_map/reduce_scatter | solution.py:294
  1595.2 30.5 %reduce-scatter.27.cloned.1.call-done = bf16[256,1024]{1,0:T(8,128)(2,1)} async-done(((bf16[1024,1024]{1,0:T(8,128)(2,1)}), bf16[256,1024]{1,0:T(8,128)(2,1)}) %reduce-scatter.27.cloned.1.call-update) | async-done | bytes 524304 | tf_op jit(solution)/shard_map/reduce_scatter | solution.py:278
  1627.4 39.7 %all-reduce.14 = (f32[1024]{0:T(1024)S(1)}, f32[1024]{0:T(1024)S(1)}, f32[1024]{0:T(1024)S(1)}, f32[1024]{0:T(1024)S(1)}, f32[1024]{0:T(1024)S(1)}, /*index=5*/f32[1024]{0:T(1024)S(1)}) all-reduce(f32[1024]{0:T(1024)S(1)} %copy-done.57, ...), channel_id=25, replica_groups=mesh['seq'=8,'tensor'=4] {'seq','tensor'}, use_global_device_ids=true, to_apply=%region_45.46.clone | all-reduce | flops 6144 | bytes 49152
  (690 shorter events, 750.0 us)
Async XLA Ops:
  7.2 159.7 %all-gather.37.cloned.1.call-start = ((), (), s32[]{:S(2)}) async-start(), calls=%async_computation.30 | async-start | bytes 1769472 | tf_op jit(solution)/shard_map/all_gather | solution.py:185
  10.0 156.9 %all-gather.29.cloned.1.call-start = ((), (), s32[]{:S(2)}) async-start(), calls=%async_computation.14 | async-start | bytes 2621440 | tf_op jit(solution)/shard_map/all_gather | solution.py:157
  60.9 118.4 %all-gather.39.cloned.1.call-start = ((), (), s32[]{:S(2)}) async-start(), calls=%async_computation.31 | async-start | bytes 2359296 | tf_op jit(solution)/shard_map/all_gather | solution.py:187
  61.8 133.4 %all-gather.41.cloned.1.call-start = ((), (), s32[]{:S(2)}) async-start(), calls=%async_computation.32 | async-start | bytes 2359296 | tf_op jit(solution)/shard_map/all_gather | solution.py:188
  62.7 256.8 %reduce-scatter.21.cloned.1.call-start = ((), (), s32[]{:S(2)}) async-start(), calls=%async_computation.15 | async-start | bytes 2621440 | tf_op jit(solution)/shard_map/reduce_scatter | solution.py:206
  266.8 153.5 %all-gather.33.cloned.1.call-start = ((), (), s32[]{:S(2)}) async-start(), calls=%async_computation.18 | async-start | bytes 2621440 | tf_op jit(solution)/shard_map/all_gather | solution.py:232
  270.0 154.1 %all-gather.43.cloned.1.call-start = ((), (), s32[]{:S(2)}) async-start(), calls=%async_computation.33 | async-start | bytes 1769472 | tf_op jit(solution)/shard_map/all_gather | solution.py:185
  270.9 153.2 %all-gather.31.cloned.1.call-start = ((), (), s32[]{:S(2)}) async-start(), calls=%async_computation.16 | async-start | bytes 2621440 | tf_op jit(solution)/shard_map/all_gather | solution.py:157
  323.8 154.9 %all-gather.45.cloned.1.call-start = ((), (), s32[]{:S(2)}) async-start(), calls=%async_computation.34 | async-start | bytes 2359296 | tf_op jit(solution)/shard_map/all_gather | solution.py:187
  324.5 212.6 %all-gather.47.cloned.1.call-start = ((), (), s32[]{:S(2)}) async-start(), calls=%async_computation.35 | async-start | bytes 2359296 | tf_op jit(solution)/shard_map/all_gather | solution.py:188
  325.1 491.5 %reduce-scatter.25.cloned.1.call-start = ((), (), s32[]{:S(2)}) async-start(), calls=%async_computation.19 | async-start | bytes 2621440 | tf_op jit(solution)/shard_map/reduce_scatter | solution.py:278
  429.2 118.0 %collective-permute-start.3 = (bf16[2,1024,4,64]{1,3,2,0:T(8,128)(2,1)S(1)}, bf16[2,1024,4,64]{1,3,2,0:T(8,128)(2,1)}, u32[]{:S(2)}, u32[]{:S(2)}) collective-permute-start(bf16[2,1024,4,64]{1,3,2,0:T(8,128)(2,1)S(1)} %pad_maximum_fusion.3), channel_id=1, source_target_pairs={{0,4},{4,8},{8,12},{12,16},{16,20},{20,24},{24,28},{1,5},{5,9},{9,... | collective-permute-start | bytes 3145736 | tf_op jit(solution)/shard_map/ppermute | solution.py:17
  433.6 113.6 %collective-permute-start.2 = (bf16[2,1024,4,64]{1,3,2,0:T(8,128)(2,1)S(1)}, bf16[2,1024,4,64]{1,3,2,0:T(8,128)(2,1)}, u32[]{:S(2)}, u32[]{:S(2)}) collective-permute-start(bf16[2,1024,4,64]{1,3,2,0:T(8,128)(2,1)S(1)} %pad_maximum_fusion.3), channel_id=1, source_target_pairs={{0,8},{4,12},{8,16},{12,20},{16,24},{20,28},{1,9},{5,13},{9,17},{1... | collective-permute-start | bytes 3145736 | tf_op jit(solution)/shard_map/ppermute | solution.py:17
  872.7 287.7 %reduce-scatter.47.cloned.1.call-start = ((), (), s32[]{:S(2)}) async-start(), calls=%async_computation.37 | async-start | bytes 73728
  873.6 287.6 %reduce-scatter.45.cloned.1.call-start = ((), (), s32[]{:S(2)}) async-start(), calls=%async_computation.36 | async-start | bytes 73728
  905.9 299.1 %reduce-scatter.35.cloned.1.call-start = ((), (), s32[]{:S(2)}) async-start(), calls=%async_computation.25 | async-start | bytes 589824 | tf_op jit(solution)/shard_map/reduce_scatter | solution.py:288
  909.3 295.7 %reduce-scatter.33.cloned.1.call-start = ((), (), s32[]{:S(2)}) async-start(), calls=%async_computation.24 | async-start | bytes 589824 | tf_op jit(solution)/shard_map/reduce_scatter | solution.py:288
  1083.4 157.6 %reduce-scatter.31.cloned.1.call-start = ((), (), s32[]{:S(2)}) async-start(), calls=%async_computation.23 | async-start | bytes 1769472 | tf_op jit(solution)/shard_map/reduce_scatter | solution.py:285
  1093.3 216.2 %reduce-scatter.29.cloned.1.call-start = ((), (), s32[]{:S(2)}) async-start(), calls=%async_computation.22 | async-start | bytes 1769472 | tf_op jit(solution)/shard_map/reduce_scatter | solution.py:285
  1126.5 253.7 %reduce-scatter.39.cloned.1.call-start = ((), (), s32[]{:S(2)}) async-start(), calls=%async_computation.27 | async-start | bytes 2359296 | tf_op jit(solution)/shard_map/reduce_scatter | solution.py:291
  1132.5 318.6 %reduce-scatter.37.cloned.1.call-start = ((), (), s32[]{:S(2)}) async-start(), calls=%async_computation.26 | async-start | bytes 2359296 | tf_op jit(solution)/shard_map/reduce_scatter | solution.py:291
  1138.6 383.4 %reduce-scatter.43.cloned.1.call-start = ((), (), s32[]{:S(2)}) async-start(), calls=%async_computation.29 | async-start | bytes 2359296 | tf_op jit(solution)/shard_map/reduce_scatter | solution.py:294
  1144.8 448.4 %reduce-scatter.41.cloned.1.call-start = ((), (), s32[]{:S(2)}) async-start(), calls=%async_computation.28 | async-start | bytes 2359296 | tf_op jit(solution)/shard_map/reduce_scatter | solution.py:294
  1150.9 474.9 %reduce-scatter.27.cloned.1.call-start = ((), (), s32[]{:S(2)}) async-start(), calls=%async_computation.21 | async-start | bytes 2621440 | tf_op jit(solution)/shard_map/reduce_scatter | solution.py:278
  (120 other events, 6362.2 us)
Sparse Core Ops, SparseCore 0:
  10.6 48.0 all-gather.36
  61.0 23.7 all-gather.28
  87.5 53.3 all-gather.38
  143.4 51.7 all-gather.40
  266.9 52.5 reduce-scatter.20
  321.5 22.5 all-gather.32
  346.7 47.9 all-gather.42
  396.9 20.5 all-gather.30
  420.2 58.3 all-gather.44
  480.6 56.4 all-gather.46
  762.9 51.2 reduce-scatter.24
  816.6 51.0 reduce-scatter.22
  872.8 22.5 all-gather.34
  899.3 62.5 reduce-scatter.46
  965.1 61.4 reduce-scatter.44
  1029.8 61.7 reduce-scatter.34
  1095.3 77.0 reduce-scatter.32
  1175.7 65.2 reduce-scatter.30
  1244.5 64.9 reduce-scatter.28
  1312.8 67.3 reduce-scatter.38
  1383.7 67.3 reduce-scatter.36
  1454.7 67.2 reduce-scatter.42
  1525.5 67.5 reduce-scatter.40
  1595.5 30.1 reduce-scatter.26
where the time goes:
time: 1690 us; the launch traced here: 1680 us
  waiting for transfers between devices  663 us (39%)
  matrix products  427 us (25%)
  blocking collectives  314 us (19%)
  other arithmetic  155 us (9%)
  local copies, waits for them, and re-layouts  80.6 us (5%)
  starting transfers between devices  19.8 us (1%)
    dot_general x56, matrix products, contract_cols(): lax.dot_general(left, right, (((1,), (1,)), ((), ())), preferred_element_...  179 us
    reduce_scatter x2, waiting for transfers between devices, local(): lax.psum_scatter(fall_grad.astype(jnp.bfloat16), 'seq', scatter_dimension...  140 us
    reduce_scatter x2, waiting for transfers between devices, local(): lax.psum_scatter(rise_weight_grad.astype(jnp.bfloat16), 'seq', scatter_di...  140 us
    unnamed x3, blocking collectives  125 us
    dot_general x40, matrix products, contract_rows(): lax.dot_general(left, right, (((0,), (0,)), ((), ())), preferred_element_...  109 us
    reduce_scatter x2, waiting for transfers between devices, local(): lax.psum_scatter(joint_weight_grad.astype(jnp.bfloat16), 'seq', scatter_d...  103 us
    reduce_scatter x2, waiting for transfers between devices, local(): lax.psum_scatter(partial_sum.astype(jnp.bfloat16), 'tensor', scatter_dime...  97.3 us
    all_gather x2, blocking collectives, local(): lax.all_gather(out_weight[layer], 'seq', axis=0, tiled=True)  66.1 us
  transfers between devices with their start and end apart: 32, of which 15 were waited for; matrix products, arithmetic and copies ran while one was open for 23% of the time, Pallas kernels for 0%

commit v1 on v0

v1 whole, which is shorter than its diff:
```python
import functools
import jax
import jax.numpy as jnp
from jax import lax
from jax.experimental import pallas as pl
from jax.experimental.pallas import tpu as pltpu
from jax.sharding import PartitionSpec as P

HEAD_DIM = 64
ROT = 16
UNIT = 512
LANES = 128
PAIR = 2 * LANES
EPSILON = 1e-05
MASKED = -1e30
BF = jnp.bfloat16
F32 = jnp.float32


def dot_nn(left, right):
    return lax.dot_general(left, right, (((1,), (0,)), ((), ())), preferred_element_type=F32)


def dot_nt(left, right):
    return lax.dot_general(left, right, (((1,), (1,)), ((), ())), preferred_element_type=F32)


def dot_tn(left, right):
    return lax.dot_general(left, right, (((0,), (0,)), ((), ())), preferred_element_type=F32)


def turned(values, cosine, sine_low, sine_high):
    ahead = pltpu.roll(values, LANES - ROT // 2, 1)
    behind = pltpu.roll(values, ROT // 2, 1)
    return values * cosine + ahead * sine_low + behind * sine_high


def turned_back(grad, cosine, sine_low, sine_high):
    ahead = pltpu.roll(grad, LANES - ROT // 2, 1)
    behind = pltpu.roll(grad, ROT // 2, 1)
    return grad * cosine - ahead * sine_low - behind * sine_high


def qkv_kernel(x_ref, w_ref, b_ref, c_ref, s1_ref, s2_ref, q_ref, kv_ref, tail_ref):
    joint = dot_nn(x_ref[...], w_ref[...]) + b_ref[...]
    cosine, low, high = c_ref[...], s1_ref[...], s2_ref[...]
    pairs = q_ref.shape[1] // LANES
    for pair in range(pairs):
        lanes = slice(pair * LANES, (pair + 1) * LANES)
        query = turned(joint[:, lanes], cosine, low, high) * HEAD_DIM**-0.5
        q_ref[:, lanes] = query.astype(BF)
        at = (pairs + pair) * LANES
        key = turned(joint[:, at : at + LANES], cosine, low, high).astype(BF)
        at = (2 * pairs + pair) * LANES
        value = joint[:, at : at + LANES].astype(BF)
        kv_ref[0, pair, :, :LANES] = key
        kv_ref[0, pair, :, LANES:] = value
        tail_ref[pair, :, :LANES] = key
        tail_ref[pair, :, LANES:] = value


def qkv_call(normed, weight, bias, tables):
    rows, width = normed.shape
    cols = weight.shape[1]
    head_width = cols // 3
    pairs = head_width // LANES
    blocks = rows // UNIT
    tile = 256
    per = UNIT // tile
    row_spec = pl.BlockSpec((tile, LANES), lambda m: (m, 0))
    first_tail = (blocks - 1) * per
    return pl.pallas_call(
        qkv_kernel,
        grid=(rows // tile,),
        in_specs=[
            pl.BlockSpec((tile, width), lambda m: (m, 0)),
            pl.BlockSpec((width, cols), lambda m: (0, 0)),
            pl.BlockSpec((1, cols), lambda m: (0, 0)),
            row_spec,
            row_spec,
            row_spec,
        ],
        out_specs=[
            pl.BlockSpec((tile, head_width), lambda m: (m, 0)),
            pl.BlockSpec((1, pairs, tile, PAIR), lambda m: (m // per, 0, m % per, 0)),
            pl.BlockSpec((pairs, tile, PAIR), lambda m: (0, jnp.maximum(m - first_tail, 0), 0)),
        ],
        out_shape=[
            jax.ShapeDtypeStruct((rows, head_width), BF),
            jax.ShapeDtypeStruct((blocks, pairs, UNIT, PAIR), BF),
            jax.ShapeDtypeStruct((pairs, UNIT, PAIR), BF),
        ],
        name="qkv",
    )(normed, weight, bias, *tables)


def fill_window(far, near, own, window, at):
    lanes = slice(at, at + LANES)
    window[0:UNIT] = far[0, :, lanes]
    for block in range(2):
        window[(1 + block) * UNIT : (2 + block) * UNIT] = near[block, 0, :, lanes]
        window[(3 + block) * UNIT : (4 + block) * UNIT] = own[block, 0, :, lanes]


def half_of(values, head):
    lane = lax.broadcasted_iota(jnp.int32, values.shape, 1)
    return jnp.where((lane >= HEAD_DIM) == bool(head), values, jnp.zeros_like(values))


def fwd_kernel(n_ref, q_ref, own_ref, near_ref, far_ref, o_ref, lse_ref, kw, vw, vt):
    fill_window(far_ref, near_ref, own_ref, kw, 0)
    fill_window(far_ref, near_ref, own_ref, vw, LANES)
    for block in range(5):
        rows = slice(block * UNIT, (block + 1) * UNIT)
        vt[:, rows] = vw[rows].T
    key_at = lax.broadcasted_iota(jnp.int32, (UNIT, UNIT), 0)
    query_at = lax.broadcasted_iota(jnp.int32, (UNIT, UNIT), 1)
    for block in range(2):
        rows = slice(block * UNIT, (block + 1) * UNIT)
        outs = []
        for head in range(2):
            query = half_of(q_ref[rows, :], head)
            part = slice(head * HEAD_DIM, (head + 1) * HEAD_DIM)
            at = (3 + block) * UNIT
            score = dot_nt(kw[at : at + UNIT], query)
            score = jnp.where(key_at <= query_at, score, MASKED)
            top = jnp.max(score, axis=0, keepdims=True)
            probs = jnp.exp(score - top)
            total = jnp.sum(probs, axis=0, keepdims=True)
            acc = dot_nn(vt[part, at : at + UNIT], probs.astype(BF))

            def step(back, carry, query=query, at=at, part=part):
                top, total, acc = carry
                where = pl.ds(pl.multiple_of(at - back * UNIT, UNIT), UNIT)
                score = dot_nt(kw[where], query)
                higher = jnp.maximum(top, jnp.max(score, axis=0, keepdims=True))
                shrink = jnp.exp(top - higher)
                probs = jnp.exp(score - higher)
                total = total * shrink + jnp.sum(probs, axis=0, keepdims=True)
                acc = acc * shrink + dot_nn(vt[part, where], probs.astype(BF))
                return higher, total, acc

            top, total, acc = lax.fori_loop(1, n_ref[block], step, (top, total, acc))
            outs.append(acc * (1.0 / total))
            lse_ref[0, head : head + 1, rows] = top + jnp.log(total)
        o_ref[rows, :] = jnp.concatenate(outs, axis=0).T.astype(BF)


def window_specs(rows, pairs):
    blocks = rows // UNIT
    kv_spec = pl.BlockSpec((blocks, 1, UNIT, PAIR), lambda p, n: (0, p, 0, 0))
    far_spec = pl.BlockSpec((1, UNIT, PAIR), lambda p, n: (p, 0, 0))
    row_spec = pl.BlockSpec((rows, LANES), lambda p, n: (0, p))
    return row_spec, kv_spec, far_spec


def fwd_call(counts, query, own, near, far):
    rows, head_width = query.shape
    pairs = head_width // LANES
    row_spec, kv_spec, far_spec = window_specs(rows, pairs)
    return pl.pallas_call(
        fwd_kernel,
        grid_spec=pltpu.PrefetchScalarGridSpec(
            num_scalar_prefetch=1,
            grid=(pairs,),
            in_specs=[row_spec, kv_spec, kv_spec, far_spec],
            out_specs=[row_spec, pl.BlockSpec((1, 2, rows), lambda p, n: (p, 0, 0))],
            scratch_shapes=[pltpu.VMEM((5 * UNIT, LANES), BF)] * 2
            + [pltpu.VMEM((LANES, 5 * UNIT), BF)],
        ),
        out_shape=[
            jax.ShapeDtypeStruct((rows, head_width), BF),
            jax.ShapeDtypeStruct((pairs, 2, rows), F32),
        ],
        name="attend",
    )(counts, query, own, near, far)


def bwd_kernel(
    n_ref, q_ref, own_ref, near_ref, far_ref, o_ref, do_ref, lse_ref, c_ref, s1_ref, s2_ref,
    dq_ref, down_ref, dnear_ref, dfar_ref, kw, vw, kt, dk, dv, dqt,
):
    fill_window(far_ref, near_ref, own_ref, kw, 0)
    fill_window(far_ref, near_ref, own_ref, vw, LANES)
    for block in range(5):
        rows = slice(block * UNIT, (block + 1) * UNIT)
        kt[:, rows] = kw[rows].T
    dk[...] = jnp.zeros_like(dk)
    dv[...] = jnp.zeros_like(dv)
    lane = lax.broadcasted_iota(jnp.int32, (UNIT, LANES), 1)
    key_at = lax.broadcasted_iota(jnp.int32, (UNIT, UNIT), 0)
    query_at = lax.broadcasted_iota(jnp.int32, (UNIT, UNIT), 1)
    for block in range(2):
        rows = slice(block * UNIT, (block + 1) * UNIT)
        grad = do_ref[rows, :]
        both = grad.astype(F32) * o_ref[rows, :].astype(F32)
        delta0 = jnp.sum(jnp.where(lane < HEAD_DIM, both, 0.0), axis=1, keepdims=True)
        delta1 = jnp.sum(jnp.where(lane < HEAD_DIM, 0.0, both), axis=1, keepdims=True)
        deltas = jnp.where(lane == 0, delta0, delta1).T
        dqt[...] = jnp.zeros_like(dqt)
        for head in range(2):
            query = half_of(q_ref[rows, :], head)
            grad_half = half_of(grad, head)
            lse = lse_ref[0, head : head + 1, rows]
            delta = deltas[head : head + 1, :]
            part = slice(head * HEAD_DIM, (head + 1) * HEAD_DIM)

            def visit(start, masked, query=query, grad_half=grad_half, lse=lse, delta=delta, part=part):
                where = pl.ds(start, UNIT)
                score = dot_nt(kw[where], query)
                if masked:
                    score = jnp.where(key_at <= query_at, score, MASKED)
                probs = jnp.exp(score - lse)
                probs_grad = dot_nt(vw[where], grad_half)
                score_grad = (probs * (probs_grad - delta)).astype(BF)
                dv[where] += dot_nn(probs.astype(BF), grad_half)
                dk[where] += dot_nn(score_grad, query)
                dqt[part, :] += dot_nn(kt[part, where], score_grad)

            at = (3 + block) * UNIT
            visit(at, True)

            def step(back, carry, at=at, visit=visit):
                visit(pl.multiple_of(at - back * UNIT, UNIT), False)
                return carry

            lax.fori_loop(1, n_ref[block], step, 0)
        dq = dqt[...].T * HEAD_DIM**-0.5
        dq_ref[rows, :] = turned_back(dq, c_ref[rows, :], s1_ref[rows, :], s2_ref[rows, :]).astype(BF)
    for source, at in ((dk, 0), (dv, LANES)):
        lanes = slice(at, at + LANES)
        dfar_ref[0, :, lanes] = source[0:UNIT].astype(BF)
        for block in range(2):
            dnear_ref[block, 0, :, lanes] = source[(1 + block) * UNIT : (2 + block) * UNIT].astype(BF)
            down_ref[block, 0, :, lanes] = source[(3 + block) * UNIT : (4 + block) * UNIT]


def bwd_call(counts, query, own, near, far, out, out_grad, lse, tables):
    rows, head_width = query.shape
    pairs = head_width // LANES
    blocks = rows // UNIT
    row_spec, kv_spec, far_spec = window_specs(rows, pairs)
    table_spec = pl.BlockSpec((rows, LANES), lambda p, n: (0, 0))
    return pl.pallas_call(
        bwd_kernel,
        grid_spec=pltpu.PrefetchScalarGridSpec(
            num_scalar_prefetch=1,
            grid=(pairs,),
            in_specs=[row_spec, kv_spec, kv_spec, far_spec, row_spec, row_spec]
            + [pl.BlockSpec((1, 2, rows), lambda p, n: (p, 0, 0))]
            + [table_spec] * 3,
            out_specs=[row_spec, kv_spec, kv_spec, far_spec],
            scratch_shapes=[pltpu.VMEM((5 * UNIT, LANES), BF)] * 2
            + [pltpu.VMEM((LANES, 5 * UNIT), BF)]
            + [pltpu.VMEM((5 * UNIT, LANES), F32)] * 2
            + [pltpu.VMEM((LANES, UNIT), F32)],
        ),
        out_shape=[
            jax.ShapeDtypeStruct((rows, head_width), BF),
            jax.ShapeDtypeStruct((blocks, pairs, UNIT, PAIR), F32),
            jax.ShapeDtypeStruct((blocks, pairs, UNIT, PAIR), BF),
            jax.ShapeDtypeStruct((pairs, UNIT, PAIR), BF),
        ],
        name="attend_back",
    )(counts, query, own, near, far, out, out_grad, lse, *tables)


def join_kernel(dq_ref, own_ref, near_ref, far_ref, c_ref, s1_ref, s2_ref, jg_ref, sum_ref):
    block = pl.program_id(0)
    cosine, low, high = c_ref[...], s1_ref[...], s2_ref[...]
    pairs = dq_ref.shape[1] // LANES
    last = (block == pl.num_programs(0) - 1).astype(F32)
    parts = [dq_ref[:, p * LANES : (p + 1) * LANES] for p in range(pairs)]
    for at in (0, LANES):
        for pair in range(pairs):
            lanes = slice(at, at + LANES)
            grad = own_ref[0, pair, :, lanes] + near_ref[0, pair, :, lanes].astype(F32)
            grad = grad + last * far_ref[pair, :, lanes].astype(F32)
            if at == 0:
                grad = turned_back(grad, cosine, low, high)
            parts.append(grad.astype(BF))
    for index, part in enumerate(parts):
        lanes = slice(index * LANES, (index + 1) * LANES)
        jg_ref[:, lanes] = part
        column = jnp.sum(part.astype(F32), axis=0, keepdims=True)

        @pl.when(block == 0)
        def _():
            sum_ref[:, lanes] = column

        @pl.when(block > 0)
        def _():
            sum_ref[:, lanes] += column


def join_call(dq, own, near, far, tables):
    rows, head_width = dq.shape
    pairs = head_width // LANES
    blocks = rows // UNIT
    table_spec = pl.BlockSpec((UNIT, LANES), lambda b: (b, 0))
    kv_spec = pl.BlockSpec((1, pairs, UNIT, PAIR), lambda b: (b, 0, 0, 0))
    return pl.pallas_call(
        join_kernel,
        grid=(blocks,),
        in_specs=[
            pl.BlockSpec((UNIT, head_width), lambda b: (b, 0)),
            kv_spec,
            kv_spec,
            pl.BlockSpec((pairs, UNIT, PAIR), lambda b: (0, 0, 0)),
        ]
        + [table_spec] * 3,
        out_specs=[
            pl.BlockSpec((UNIT, 3 * head_width), lambda b: (b, 0)),
            pl.BlockSpec((1, 3 * head_width), lambda b: (0, 0)),
        ],
        out_shape=[
            jax.ShapeDtypeStruct((rows, 3 * head_width), BF),
            jax.ShapeDtypeStruct((1, 3 * head_width), F32),
        ],
        name="join",
    )(dq, own, near, far, *tables)


def up_kernel(x_ref, w_ref, b_ref, hidden_ref, slope_ref):
    rise = dot_nn(x_ref[...], w_ref[...]) + b_ref[...]
    phi = 0.5 + 0.5 * lax.erf(rise * 0.7071067811865476)
    bell = jnp.exp(rise * rise * -0.5) * 0.3989422804014327
    hidden_ref[...] = (rise * phi).astype(BF)
    slope_ref[...] = phi + rise * bell


def up_call(normed, weight, bias):
    rows, width = normed.shape
    cols = weight.shape[1]
    tile = 256
    return pl.pallas_call(
        up_kernel,
        grid=(rows // tile,),
        in_specs=[
            pl.BlockSpec((tile, width), lambda m: (m, 0)),
            pl.BlockSpec((width, cols), lambda m: (0, 0)),
            pl.BlockSpec((1, cols), lambda m: (0, 0)),
        ],
        out_specs=[pl.BlockSpec((tile, cols), lambda m: (m, 0))] * 2,
        out_shape=[
            jax.ShapeDtypeStruct((rows, cols), BF),
            jax.ShapeDtypeStruct((rows, cols), F32),
        ],
        name="up",
    )(normed, weight, bias)


def flipped(count, bit):
    return [(i, i ^ bit) for i in range(count)]


def shifted(count, distance):
    devices = range(count)
    return [(i - distance, i) for i in devices if i - distance in devices]


def rolled_outer(outer, distance):
    return [
        (o * 2 + y, (o + distance) % outer * 2 + y) for o in range(outer) for y in range(2)
    ]


def gather_rows(piece):
    count = lax.axis_size("seq")
    outer = count // 2
    place = lax.axis_index("seq")
    at, side = place // 2, place % 2
    chunk, cols = piece.shape
    line = jnp.zeros((outer, chunk, cols), piece.dtype)
    line = lax.dynamic_update_index_in_dim(line, piece, at, 0)
    for distance in range(1, outer):
        came = lax.ppermute(piece, "seq", rolled_outer(outer, distance))
        line = lax.dynamic_update_index_in_dim(line, came, (at - distance) % outer, 0)
    other = lax.ppermute(line, "seq", flipped(count, 1))
    full = jnp.zeros((outer, 2, chunk, cols), piece.dtype)
    full = lax.dynamic_update_index_in_dim(full, line, side, 1)
    full = lax.dynamic_update_index_in_dim(full, other, 1 - side, 1)
    return full.reshape(count * chunk, cols)


def gather_rows_whole(piece):
    return lax.all_gather(piece, "seq", axis=0, tiled=True)


def halves(values):
    count = lax.axis_size("seq")
    side = lax.axis_index("seq") % 2
    rows, width = values.shape
    split = values.reshape(rows, count // 2, 2, width // count)
    mine = lax.dynamic_index_in_dim(split, side, 2, keepdims=False)
    other = lax.dynamic_index_in_dim(split, 1 - side, 2, keepdims=False)
    return mine.reshape(rows, width // 2), other.reshape(rows, width // 2)


def scatter_grad(left, right):
    count = lax.axis_size("seq")
    outer = count // 2
    at = lax.axis_index("seq") // 2
    mine, other = left
    sent = dot_tn(other, right).astype(BF)
    came = lax.ppermute(sent, "seq", flipped(count, 1))
    paired = (dot_tn(mine, right) + came.astype(F32)).astype(BF)
    line = paired.reshape(outer, -1, right.shape[1])
    total = lax.dynamic_index_in_dim(line, at, 0, keepdims=False).astype(F32)
    for distance in range(1, outer):
        part = lax.dynamic_index_in_dim(line, (at + distance) % outer, 0, keepdims=False)
        part = lax.ppermute(part, "seq", rolled_outer(outer, distance))
        total = total + part.astype(F32)
    return total


def gather_tokens(rows):
    count = lax.axis_size("tensor")
    me = lax.axis_index("tensor")
    across = lax.ppermute(rows, "tensor", flipped(count, 2))
    beside = lax.ppermute(rows, "tensor", flipped(count, 1))
    diagonal = lax.ppermute(across, "tensor", flipped(count, 1))
    out = jnp.zeros((count,) + rows.shape, rows.dtype)
    out = lax.dynamic_update_index_in_dim(out, rows, me, 0)
    out = lax.dynamic_update_index_in_dim(out, beside, me ^ 1, 0)
    out = lax.dynamic_update_index_in_dim(out, across, me ^ 2, 0)
    out = lax.dynamic_update_index_in_dim(out, diagonal, me ^ 3, 0)
    return out.reshape(count * rows.shape[0], rows.shape[1])


def scatter_tokens(partial):
    count = lax.axis_size("tensor")
    me = lax.axis_index("tensor")
    core, chip = me % 2, me // 2
    split = partial.reshape(2, 2, partial.shape[0] // count, partial.shape[1])
    sent = lax.dynamic_index_in_dim(split, 1 - core, 1, keepdims=False)
    kept = lax.dynamic_index_in_dim(split, core, 1, keepdims=False)
    came = lax.ppermute(sent, "tensor", flipped(count, 1))
    far = lax.dynamic_index_in_dim(kept, 1 - chip, 0, keepdims=False).astype(F32)
    far = far + lax.dynamic_index_in_dim(came, 1 - chip, 0, keepdims=False).astype(F32)
    across = lax.ppermute(far.astype(BF), "tensor", flipped(count, 2))
    near = lax.dynamic_index_in_dim(kept, chip, 0, keepdims=False).astype(F32)
    near = near + lax.dynamic_index_in_dim(came, chip, 0, keepdims=False).astype(F32)
    return near + across.astype(F32)


def exchanged(rows):
    return lax.all_to_all(rows, ("seq", "tensor"), 0, 0, tiled=True)


def layer_norm(values, gain, shift):
    center = values - jnp.mean(values, axis=1, keepdims=True)
    scale_inv = lax.rsqrt(jnp.mean(center * center, axis=1, keepdims=True) + EPSILON)
    unit = center * scale_inv
    return (unit * gain + shift, unit, scale_inv)


def norm_back(grad, unit, scale_inv, gain):
    scaled = grad * gain
    return scale_inv * (
        scaled
        - jnp.mean(scaled, axis=1, keepdims=True)
        - unit * jnp.mean(scaled * unit, axis=1, keepdims=True)
    )


def rotary_tables(offsets):
    exponent = jnp.arange(0, ROT, 2).astype(F32) / ROT
    rates = 10000.0 ** (-exponent)
    head = jnp.concatenate([rates, rates, jnp.zeros(HEAD_DIM - ROT, F32)])
    lane = jnp.arange(LANES) % HEAD_DIM
    angles = offsets.astype(F32)[:, None] * jnp.concatenate([head, head])[None, :]
    sine = jnp.sin(angles)
    low = jnp.where(lane < ROT // 2, -sine, 0.0)
    high = jnp.where((lane >= ROT // 2) & (lane < ROT), sine, 0.0)
    return (jnp.cos(angles), low, high)


def local(
    block_input,
    lengths,
    ln_gain,
    ln_bias,
    qkv_weight,
    qkv_bias,
    out_weight,
    up_weight,
    up_bias,
    down_weight,
    out_bias,
    out_grad,
):
    tensor_count = lax.axis_size("tensor")
    seq_count = lax.axis_size("seq")
    everyone = seq_count * tensor_count
    me_tensor = lax.axis_index("tensor")
    own_rows, width = block_input.shape
    group = own_rows * tensor_count
    layers = qkv_weight.shape[0]
    chunk = qkv_weight.shape[1]
    head_width = qkv_weight.shape[3]
    heads = head_width // HEAD_DIM
    hidden_width = up_weight.shape[2]
    first = lax.axis_index("seq") * group
    positions = first + jnp.arange(group, dtype=jnp.int32)
    ends = jnp.cumsum(lengths)
    starts_of = jnp.sum(jnp.where(ends[None, :] <= positions[:, None], lengths[None, :], 0), axis=1)
    offsets = positions - starts_of
    tables = rotary_tables(offsets)
    counts = offsets[::UNIT] // UNIT + 1

    small_sizes = []
    pieces = []
    for array in (ln_gain, ln_bias, out_bias, qkv_bias, up_bias):
        pieces.append(array.reshape(-1))
        small_sizes.append(array.size)
    packed = jnp.concatenate(pieces)
    small = exchanged(jnp.broadcast_to(packed[None, :], (everyone, packed.size)))
    parts = []
    at = 0
    for size in small_sizes:
        parts.append(small[:, at : at + size])
        at += size

    def over_all(part):
        return jnp.transpose(part.reshape(everyone, layers, -1), (1, 0, 2)).reshape(layers, width)

    def over_seq(part):
        part = part.reshape(seq_count, tensor_count, -1)
        return lax.dynamic_index_in_dim(part, me_tensor, 1, keepdims=False)

    gains = over_all(parts[0]).astype(F32)
    shifts = over_all(parts[1]).astype(F32)
    out_biases = over_all(parts[2]).astype(F32)
    per = HEAD_DIM // seq_count
    joint_bias = over_seq(parts[3]).reshape(seq_count, layers, 3, heads, per)
    joint_bias = jnp.transpose(joint_bias, (1, 2, 3, 0, 4)).reshape(layers, 1, 3 * head_width)
    joint_bias = joint_bias.astype(F32)
    groups = up_bias.shape[1]
    rise_bias = over_seq(parts[4]).reshape(seq_count, layers, groups, -1)
    rise_bias = jnp.transpose(rise_bias, (1, 2, 0, 3)).reshape(layers, 1, hidden_width).astype(F32)

    weights = []
    for layer in range(layers):
        gather = GATHER[layer]
        weights.append(
            (
                gather(qkv_weight[layer].reshape(chunk, 3 * head_width)),
                gather(up_weight[layer]),
                gather(jnp.concatenate([out_weight[layer], down_weight[layer]], axis=1)),
            )
        )

    kept = []
    current = block_input
    for layer in range(layers):
        qkv_full, up_full, fall_full = weights[layer]
        normed, unit, scale_inv = layer_norm(current, gains[layer][None], shifts[layer][None])
        normed_rows = gather_tokens(normed.astype(BF))
        query, own, tail = qkv_call(normed_rows, qkv_full, joint_bias[layer], tables)
        near = lax.ppermute(own, "seq", shifted(seq_count, 1))
        far = lax.ppermute(tail, "seq", shifted(seq_count, 2))
        hidden, slope = up_call(normed_rows, up_full, rise_bias[layer])
        mixed, lse = fwd_call(counts, query, own, near, far)
        partial = dot_nt(mixed, fall_full[:, :head_width]) + dot_nt(hidden, fall_full[:, head_width:])
        branch = scatter_tokens(partial.astype(BF))
        kept.append((normed_rows, unit, scale_inv, query, own, near, far, hidden, slope, mixed, lse))
        current = current + branch + out_biases[layer][None, :]

    gradient = out_grad
    collected = []
    for layer in reversed(range(layers)):
        qkv_full, up_full, fall_full = weights[layer]
        normed_rows, unit, scale_inv, query, own, near, far, hidden, slope, mixed, lse = kept[layer]
        bias_grad = jnp.sum(gradient, axis=0)
        grad_rows = gather_tokens(gradient.astype(BF))
        grad_halves = halves(grad_rows)
        normed_halves = halves(normed_rows)
        mixed_grad = dot_nn(grad_rows, fall_full[:, :head_width]).astype(BF)
        fall_grad = scatter_grad(grad_halves, jnp.concatenate([mixed, hidden], axis=1))
        dq, down, dnear, dfar = bwd_call(counts, query, own, near, far, mixed, mixed_grad, lse, tables)
        came_near = lax.ppermute(dnear, "seq", shifted(seq_count, -1))
        came_far = lax.ppermute(dfar, "seq", shifted(seq_count, -2))
        hidden_grad = dot_nn(grad_rows, fall_full[:, head_width:])
        rise_grad = (hidden_grad * slope).astype(BF)
        rise_bias_grad = jnp.sum(rise_grad, axis=0, dtype=F32)
        up_grad = scatter_grad(normed_halves, rise_grad)
        normed_part = dot_nt(rise_grad, up_full)
        joint_grad, joint_bias_grad = join_call(dq, down, came_near, came_far, tables)
        joint_weight_grad = scatter_grad(normed_halves, joint_grad)
        normed_part = normed_part + dot_nt(joint_grad, qkv_full)
        normed_grad = scatter_tokens(normed_part.astype(BF))
        gain_grad = jnp.sum(normed_grad * unit, axis=0)
        shift_grad = jnp.sum(normed_grad, axis=0)
        gradient = gradient + norm_back(normed_grad, unit, scale_inv, gains[layer][None, :])
        collected.append(
            (gain_grad, shift_grad, bias_grad, joint_bias_grad.reshape(-1), rise_bias_grad,
             joint_weight_grad, fall_grad, up_grad)
        )
    collected = collected[::-1]

    def stacked(member):
        return jnp.stack([entry[member] for entry in collected])

    def to_all(member):
        value = stacked(member).reshape(layers, everyone, -1)
        return jnp.transpose(value, (1, 0, 2)).reshape(everyone, -1)

    def to_seq(value):
        mine = jnp.arange(tensor_count)[None, :, None] == me_tensor
        return jnp.where(mine, value[:, None, :], 0.0).reshape(everyone, -1)

    joint_out = stacked(3).reshape(layers, 3, heads, seq_count, per)
    joint_out = jnp.transpose(joint_out, (3, 0, 1, 2, 4)).reshape(seq_count, -1)
    rise_out = stacked(4).reshape(layers, groups, seq_count, -1)
    rise_out = jnp.transpose(rise_out, (2, 0, 1, 3)).reshape(seq_count, -1)
    outgoing = jnp.concatenate(
        [to_all(0), to_all(1), to_all(2), to_seq(joint_out), to_seq(rise_out)], axis=1
    )
    summed = jnp.sum(exchanged(outgoing), axis=0)
    results = []
    at = 0
    for array in (ln_gain, ln_bias, out_bias, qkv_bias, up_bias):
        results.append(summed[at : at + array.size].reshape(array.shape))
        at += array.size
    joint_weight_grad = stacked(5).reshape(layers, chunk, 3, head_width)
    fall_grad = stacked(6)
    return (
        current,
        gradient,
        results[0],
        results[1],
        joint_weight_grad,
        results[3],
        fall_grad[:, :, :head_width],
        stacked(7),
        results[4],
        fall_grad[:, :, head_width:],
        results[2],
    )


GATHER = (gather_rows, gather_rows)


def solution(mesh):
    tokens = P(("seq", "tensor"), None)
    vector = P(None, ("seq", "tensor"))
    matrix = P(None, "seq", "tensor")
    joint = P(None, "seq", None, "tensor")
    joint_vector = P(None, None, "tensor", "seq")
    rise_vector = P(None, "tensor", "seq")
    in_specs = (
        tokens, P(), vector, vector, joint, joint_vector, matrix, matrix, rise_vector, matrix,
        vector, tokens,
    )
    out_specs = (
        tokens, tokens, vector, vector, joint, joint_vector, matrix, matrix, rise_vector, matrix,
        vector,
    )
    return jax.shard_map(local, mesh=mesh, in_specs=in_specs, out_specs=out_specs, check_vma=False)
```

time: 1690 us -> 858 us (0.51)
  waiting for transfers between devices: 663 us -> 250 us
  matrix products: 427 us -> 81.6 us
  blocking collectives: 314 us -> 0 us
  starting transfers between devices: 19.8 us -> 179 us
  local copies, waits for them, and re-layouts: 80.6 us -> 203 us
  other arithmetic: 155 us -> 43.5 us
  Pallas kernels: 0 us -> 89.7 us
    reduce_scatter x12 -> x0, waiting for transfers between devices: 510 us -> none  [the longest x2 140 us: local(): lax.psum_scatter(fall_grad.astype(jnp.bfloat16), 'seq', scatter_dimension...]
    dot_general x152 -> x24, matrix products: 427 us -> 81.6 us  [the longest x12 30.5 us: dot_tn(): lax.dot_general(left, right, (((0,), (0,)), ((), ())), preferred_element_...]
    ppermute x8 -> x76, waiting for transfers between devices: 43.1 us -> 244 us  [the longest x18 64.3 us: scatter_grad(): part = lax.ppermute(part, 'seq', rolled_outer(outer, distance))]
    all_gather x6 -> x0, blocking collectives: 189 us -> none  [the longest x2 66.1 us: local(): lax.all_gather(out_weight[layer], 'seq', axis=0, tiled=True)]
    ppermute x8 -> x76, starting transfers between devices: 18.7 us -> 169 us  [the longest x6 42.6 us: scatter_grad(): came = lax.ppermute(sent, 'seq', flipped(count, 1))]
    unnamed x3 -> x0, blocking collectives: 125 us -> none
    all_gather x10 -> x0, waiting for transfers between devices: 108 us -> none  [the longest x2 44.5 us: local(): lax.all_gather(down_weight[layer], 'seq', axis=0, tiled=True)]
    pallas_call x0 -> x10, Pallas kernels: none -> 89.7 us  [the longest x2 29.8 us: bwd_call(): pl.pallas_call(bwd_kernel, grid_spec=pltpu.PrefetchScalarGridSpec(num_sca...]
  transfers between devices with their start and end apart: 32 -> 78, of which waited for: 15 -> 21; matrix products, arithmetic and copies ran while one was open for 23% -> 35% of each run, Pallas kernels for 0% -> 8%
where the time goes in v1:
time: 858 us; the launch traced here: 850 us
  waiting for transfers between devices  250 us (29%)
  local copies, waits for them, and re-layouts  203 us (24%)
  starting transfers between devices  179 us (21%)
  Pallas kernels  89.7 us (10%)
  matrix products  81.6 us (10%)
  other arithmetic  43.5 us (5%)
    ppermute x18, waiting for transfers between devices, scatter_grad(): part = lax.ppermute(part, 'seq', rolled_outer(outer, distance))  64.3 us
    ppermute x6, waiting for transfers between devices, scatter_grad(): came = lax.ppermute(sent, 'seq', flipped(count, 1))  43.6 us
    ppermute x6, starting transfers between devices, scatter_grad(): came = lax.ppermute(sent, 'seq', flipped(count, 1))  42.6 us
    ppermute x6, waiting for transfers between devices, gather_rows(): other = lax.ppermute(line, 'seq', flipped(count, 1))  38.2 us
    ppermute x18, starting transfers between devices, gather_rows(): came = lax.ppermute(piece, 'seq', rolled_outer(outer, distance))  37.4 us
    ppermute x18, waiting for transfers between devices, gather_rows(): came = lax.ppermute(piece, 'seq', rolled_outer(outer, distance))  36.9 us
    dynamic_slice x6, local copies, waits for them, and re-layouts, halves(): other = lax.dynamic_index_in_dim(split, 1 - side, 2, keepdims=False)  34.7 us
    dynamic_slice x6, local copies, waits for them, and re-layouts, halves(): mine = lax.dynamic_index_in_dim(split, side, 2, keepdims=False)  33.7 us
  transfers between devices with their start and end apart: 78, of which 21 were waited for; matrix products, arithmetic and copies ran while one was open for 35% of the time, Pallas kernels for 8%

profile of v1, /device:TPU:0, one launch (start us, length us, event | category | flops | bytes accessed | tf_op | source)
XLA Modules:
  0.0 849.7 jit_solution(2436826063384683774)
XLA Ops:
  88.3 10.1 %collective-permute-start.33 = (bf16[128,1024]{1,0:T(8,128)(2,1)S(1)}, bf16[128,1024]{1,0:T(8,128)(2,1)S(1)}, u32[]{:S(2)}, u32[]{:S(2)}) collective-permute-start(bf16[128,1024]{1,0:T(8,128)(2,1)S(1)} %copy-done.60), channel_id=1, source_target_pairs={{0,16},{4,20},{8,24},{12,28},{16,0},{20,4},{24,8},{28,12},{1,17},{... | collective-permute-start | bytes 786440 | tf_op jit(solution)/shard_map/ppermute | solution.py:377
  107.7 22.0 %collective-permute-done.33 = bf16[128,1024]{1,0:T(8,128)(2,1)S(1)} collective-permute-done((bf16[128,1024]{1,0:T(8,128)(2,1)S(1)}, bf16[128,1024]{1,0:T(8,128)(2,1)S(1)}, u32[]{:S(2)}, u32[]{:S(2)}) %collective-permute-start.33) | collective-permute-done | bytes 262176 | tf_op jit(solution)/shard_map/ppermute | solution.py:377
  150.0 8.0 collective-permute-done.29
  167.2 11.5 %collective-permute-done.6 = bf16[4,128,768]{2,1,0:T(8,128)(2,1)S(1)} collective-permute-done((bf16[4,128,768]{2,1,0:T(8,128)(2,1)}, bf16[4,128,768]{2,1,0:T(8,128)(2,1)S(1)}, u32[]{:S(2)}, u32[]{:S(2)}) %collective-permute-start.6) | collective-permute-done | bytes 786464 | tf_op jit(solution)/shard_map/ppermute | solution.py:379
  188.8 12.4 %collective-permute-done.16 = bf16[4,128,1024]{2,1,0:T(8,128)(2,1)} collective-permute-done((bf16[4,128,1024]{2,1,0:T(8,128)(2,1)}, bf16[4,128,1024]{2,1,0:T(8,128)(2,1)}, u32[]{:S(2)}, u32[]{:S(2)}) %collective-permute-start.16) | collective-permute-done | bytes 1048608 | tf_op jit(solution)/shard_map/ppermute | solution.py:379
  207.2 7.9 up.2
  215.0 14.3 %collective-permute-done.12 = bf16[4,128,1280]{2,1,0:T(8,128)(2,1)} collective-permute-done((bf16[4,128,1280]{2,1,0:T(8,128)(2,1)}, bf16[4,128,1280]{2,1,0:T(8,128)(2,1)}, u32[]{:S(2)}, u32[]{:S(2)}) %collective-permute-start.12) | collective-permute-done | bytes 1310752 | tf_op jit(solution)/shard_map/ppermute | solution.py:379
  229.3 27.8 %collective-permute-start.8 = (bf16[2,512,256]{2,1,0:T(8,128)(2,1)S(1)}, bf16[2,512,256]{2,1,0:T(8,128)(2,1)S(1)}, u32[]{:S(2)}, u32[]{:S(2)}) collective-permute-start(bf16[2,512,256]{2,1,0:T(8,128)(2,1)S(1)} %copy-done.93), channel_id=1, source_target_pairs={{0,8},{4,12},{8,16},{12,20},{16,24},{20,28},{1,9},{5,13},{9,17},{1... | collective-permute-start | bytes 1572872 | tf_op jit(solution)/shard_map/ppermute | solution.py:562
  265.7 24.4 %collective-permute-done.7.near_ref = bf16[2,2,512,256]{3,2,1,0:T(8,128)(2,1)S(1)} collective-permute-done((bf16[2,2,512,256]{3,2,1,0:T(8,128)(2,1)}, bf16[2,2,512,256]{3,2,1,0:T(8,128)(2,1)S(1)}, u32[]{:S(2)}, u32[]{:S(2)}) %collective-permute-start.7) | collective-permute-done | bytes 1048608 | tf_op jit(solution)/shard_map/ppermute | solution.py:561
  291.1 10.4 %attend.2 = (bf16[1024,256]{1,0:T(8,128)(2,1)}, f32[2,2,1024]{2,1,0:T(2,128)}) custom-call(s32[2]{0:T(128)} %fusion.44.n_ref, bf16[1024,256]{1,0:T(8,128)(2,1)} %get-tuple-element.37.q_ref, bf16[2,2,512,256]{3,2,1,0:T(8,128)(2,1)} %get-tuple-element.38.own_ref, bf16[2,2,512,256]{3,2,1,0:T(8,128)(2,1)} %copy-done.26, bf16[2,512,256]{2,1,0:T(8,128)(2,1)} %copy-done.38), custom_call_target="tpu_custom_call" | custom-call | tf_op jit(solution)/shard_map/attend/pallas_call | solution.py:161
  387.5 16.0 %collective-permute-start.26 = (bf16[2,2,512,256]{3,2,1,0:T(8,128)(2,1)}, bf16[2,2,512,256]{3,2,1,0:T(8,128)(2,1)}, u32[]{:S(2)}, u32[]{:S(2)}) collective-permute-start(bf16[2,2,512,256]{3,2,1,0:T(8,128)(2,1)} %get-tuple-element.43.own_ref), channel_id=1, source_target_pairs={{0,4},{4,8},{8,12},{12,16},{16,20},{20,24},{24,28},{1,5},{5,9},{9,... | collective-permute-start | bytes 3145736 | tf_op jit(solution)/shard_map/ppermute | solution.py:561
  405.6 8.0 up.3
  446.0 10.7 %attend.3 = (bf16[1024,256]{1,0:T(8,128)(2,1)}, f32[2,2,1024]{2,1,0:T(2,128)}) custom-call(s32[2]{0:T(128)} %fusion.44.n_ref, bf16[1024,256]{1,0:T(8,128)(2,1)} %get-tuple-element.42.q_ref, bf16[2,2,512,256]{3,2,1,0:T(8,128)(2,1)} %get-tuple-element.43.own_ref, bf16[2,2,512,256]{3,2,1,0:T(8,128)(2,1)} %collective-permute-done.26.near_ref, ...), custom_call_target="tpu_custom_call" | custom-call | tf_op jit(solution)/shard_map/attend/pallas_call | solution.py:161
  456.7 14.9 %attend_back.2 = (bf16[1024,256]{1,0:T(8,128)(2,1)}, f32[2,2,512,256]{3,2,1,0:T(8,128)}, bf16[2,2,512,256]{3,2,1,0:T(8,128)(2,1)}, bf16[2,512,256]{2,1,0:T(8,128)(2,1)}) custom-call(s32[2]{0:T(128)} %fusion.44.n_ref, bf16[1024,256]{1,0:T(8,128)(2,1)} %get-tuple-element.42.q_ref, bf16[2,2,512,256]{3,2,1,0:T(8,128)(2,1)} %get-tuple-element.43.own_ref, ...), custom_call_target="tpu_custom_call" | custom-call | tf_op jit(solution)/shard_map/attend_back/pallas_call | solution.py:244
  485.0 25.7 %collective-permute-start.64 = (bf16[512,1280]{1,0:T(8,128)(2,1)}, bf16[512,1280]{1,0:T(8,128)(2,1)}, u32[]{:S(2)}, u32[]{:S(2)}) collective-permute-start(bf16[512,1280]{1,0:T(8,128)(2,1)} %convolution_convert_fusion), channel_id=1, source_target_pairs={{0,4},{4,0},{8,12},{12,8},{16,20},{20,16},{24,28},{28,24},{1,5},{5... | collective-permute-start | bytes 3932168 | tf_op jit(solution)/shard_map/ppermute | solution.py:406
  515.0 20.6 %collective-permute-done.42.far_ref = bf16[2,512,256]{2,1,0:T(8,128)(2,1)} collective-permute-done((bf16[2,512,256]{2,1,0:T(8,128)(2,1)}, bf16[2,512,256]{2,1,0:T(8,128)(2,1)}, u32[]{:S(2)}, u32[]{:S(2)}) %collective-permute-start.42) | collective-permute-done | bytes 524320 | tf_op jit(solution)/shard_map/ppermute | solution.py:583
  565.3 12.7 %collective-permute-done.56 = bf16[512,768]{1,0:T(8,128)(2,1)S(1)} collective-permute-done((bf16[512,768]{1,0:T(8,128)(2,1)S(1)}, bf16[512,768]{1,0:T(8,128)(2,1)S(1)}, u32[]{:S(2)}, u32[]{:S(2)}) %collective-permute-start.56) | collective-permute-done | bytes 786464 | tf_op jit(solution)/shard_map/ppermute | solution.py:406
  595.2 8.5 %collective-permute-done.66 = bf16[128,1280]{1,0:T(8,128)(2,1)} collective-permute-done((bf16[128,1280]{1,0:T(8,128)(2,1)}, bf16[128,1280]{1,0:T(8,128)(2,1)}, u32[]{:S(2)}, u32[]{:S(2)}) %collective-permute-start.66) | collective-permute-done | bytes 327712 | tf_op jit(solution)/shard_map/ppermute | solution.py:412
  629.6 14.9 %attend_back.3 = (bf16[1024,256]{1,0:T(8,128)(2,1)}, f32[2,2,512,256]{3,2,1,0:T(8,128)}, bf16[2,2,512,256]{3,2,1,0:T(8,128)(2,1)}, bf16[2,512,256]{2,1,0:T(8,128)(2,1)}) custom-call(s32[2]{0:T(128)} %fusion.44.n_ref, bf16[1024,256]{1,0:T(8,128)(2,1)} %get-tuple-element.37.q_ref, bf16[2,2,512,256]{3,2,1,0:T(8,128)(2,1)} %get-tuple-element.38.own_ref, ...), custom_call_target="tpu_custom_call" | custom-call | tf_op jit(solution)/shard_map/attend_back/pallas_call | solution.py:244
  682.5 15.0 %collective-permute-start.60 = (bf16[512,1280]{1,0:T(8,128)(2,1)}, bf16[512,1280]{1,0:T(8,128)(2,1)}, u32[]{:S(2)}, u32[]{:S(2)}) collective-permute-start(bf16[512,1280]{1,0:T(8,128)(2,1)} %convolution_convert_fusion.1), channel_id=1, source_target_pairs={{0,4},{4,0},{8,12},{12,8},{16,20},{20,16},{24,28},{28,24},{1,5},{5... | collective-permute-start | bytes 3932168 | tf_op jit(solution)/shard_map/ppermute | solution.py:406
  719.0 30.9 %collective-permute-done.68 = bf16[512,1024]{1,0:T(8,128)(2,1)} collective-permute-done((bf16[512,1024]{1,0:T(8,128)(2,1)}, bf16[512,1024]{1,0:T(8,128)(2,1)}, u32[]{:S(2)}, u32[]{:S(2)}) %collective-permute-start.68) | collective-permute-done | bytes 1048608 | tf_op jit(solution)/shard_map/ppermute | solution.py:406
  766.4 18.8 %collective-permute-done.70 = bf16[128,1024]{1,0:T(8,128)(2,1)S(1)} collective-permute-done((bf16[128,1024]{1,0:T(8,128)(2,1)S(1)}, bf16[128,1024]{1,0:T(8,128)(2,1)S(1)}, u32[]{:S(2)}, u32[]{:S(2)}) %collective-permute-start.70) | collective-permute-done | bytes 262176 | tf_op jit(solution)/shard_map/ppermute | solution.py:412
  788.9 19.1 %collective-permute-done.62 = bf16[128,1280]{1,0:T(8,128)(2,1)S(1)} collective-permute-done((bf16[128,1280]{1,0:T(8,128)(2,1)S(1)}, bf16[128,1280]{1,0:T(8,128)(2,1)S(1)}, u32[]{:S(2)}, u32[]{:S(2)}) %collective-permute-start.62) | collective-permute-done | bytes 327712 | tf_op jit(solution)/shard_map/ppermute | solution.py:412
  818.5 9.1 %collective-permute-done.54 = bf16[128,768]{0,1:T(8,128)(2,1)S(1)} collective-permute-done((bf16[128,768]{0,1:T(8,128)(2,1)}, bf16[128,768]{0,1:T(8,128)(2,1)S(1)}, u32[]{:S(2)}, u32[]{:S(2)}) %collective-permute-start.54) | collective-permute-done | bytes 196640 | tf_op jit(solution)/shard_map/ppermute | solution.py:412
  (612 shorter events, 473.0 us)
Async XLA Ops:
  5.1 52.6 %collective-permute-start.4 = (bf16[128,768]{0,1:T(8,128)(2,1)S(1)}, bf16[128,768]{0,1:T(8,128)(2,1)}, u32[]{:S(2)}, u32[]{:S(2)}) collective-permute-start(bf16[128,768]{0,1:T(8,128)(2,1)S(1)} %bitcast.406), channel_id=1, source_target_pairs={{0,16},{4,20},{8,24},{12,28},{16,0},{20,4},{24,8},{28,12},{1,17},{... | collective-permute-start | bytes 589832 | tf_op jit(solution)/shard_map/ppermute | solution.py:377
  7.7 51.7 %collective-permute-start.5 = (bf16[128,768]{0,1:T(8,128)(2,1)S(1)}, bf16[128,768]{0,1:T(8,128)(2,1)}, u32[]{:S(2)}, u32[]{:S(2)}) collective-permute-start(bf16[128,768]{0,1:T(8,128)(2,1)S(1)} %bitcast.407), channel_id=1, source_target_pairs={{0,24},{4,28},{8,0},{12,4},{16,8},{20,12},{24,16},{28,20},{1,25},{... | collective-permute-start | bytes 589832 | tf_op jit(solution)/shard_map/ppermute | solution.py:377
  9.2 53.1 %collective-permute-start.22 = (bf16[128,768]{0,1:T(8,128)(2,1)S(1)}, bf16[128,768]{0,1:T(8,128)(2,1)}, u32[]{:S(2)}, u32[]{:S(2)}) collective-permute-start(bf16[128,768]{0,1:T(8,128)(2,1)S(1)} %bitcast.401), channel_id=1, source_target_pairs={{0,8},{4,12},{8,16},{12,20},{16,24},{20,28},{24,0},{28,4},{1,9},{5... | collective-permute-start | bytes 589832 | tf_op jit(solution)/shard_map/ppermute | solution.py:377
  9.9 56.9 %collective-permute-start.23 = (bf16[128,768]{0,1:T(8,128)(2,1)S(1)}, bf16[128,768]{0,1:T(8,128)(2,1)}, u32[]{:S(2)}, u32[]{:S(2)}) collective-permute-start(bf16[128,768]{0,1:T(8,128)(2,1)S(1)} %bitcast.402), channel_id=1, source_target_pairs={{0,16},{4,20},{8,24},{12,28},{16,0},{20,4},{24,8},{28,12},{1,17},{... | collective-permute-start | bytes 589832 | tf_op jit(solution)/shard_map/ppermute | solution.py:377
  66.7 74.3 %collective-permute-start.9 = (bf16[128,1280]{1,0:T(8,128)(2,1)}, bf16[128,1280]{1,0:T(8,128)(2,1)}, u32[]{:S(2)}, u32[]{:S(2)}) collective-permute-start(bf16[128,1280]{1,0:T(8,128)(2,1)} %pad_maximum_fusion.3), channel_id=1, source_target_pairs={{0,8},{4,12},{8,16},{12,20},{16,24},{20,28},{24,0},{28,4},{1,9},{5... | collective-permute-start | bytes 983048 | tf_op jit(solution)/shard_map/ppermute | solution.py:377
  69.0 74.1 %collective-permute-start.10 = (bf16[128,1280]{1,0:T(8,128)(2,1)}, bf16[128,1280]{1,0:T(8,128)(2,1)}, u32[]{:S(2)}, u32[]{:S(2)}) collective-permute-start(bf16[128,1280]{1,0:T(8,128)(2,1)} %pad_maximum_fusion.3), channel_id=1, source_target_pairs={{0,16},{4,20},{8,24},{12,28},{16,0},{20,4},{24,8},{28,12},{1,17},{... | collective-permute-start | bytes 983048 | tf_op jit(solution)/shard_map/ppermute | solution.py:377
  81.9 62.9 %collective-permute-start.11 = (bf16[128,1280]{1,0:T(8,128)(2,1)S(1)}, bf16[128,1280]{1,0:T(8,128)(2,1)S(1)}, u32[]{:S(2)}, u32[]{:S(2)}) collective-permute-start(bf16[128,1280]{1,0:T(8,128)(2,1)S(1)} %copy-done.58), channel_id=1, source_target_pairs={{0,24},{4,28},{8,0},{12,4},{16,8},{20,12},{24,16},{28,20},{1,25},{... | collective-permute-start | bytes 983048 | tf_op jit(solution)/shard_map/ppermute | solution.py:377
  163.2 66.1 %collective-permute-start.12 = (bf16[4,128,1280]{2,1,0:T(8,128)(2,1)}, bf16[4,128,1280]{2,1,0:T(8,128)(2,1)}, u32[]{:S(2)}, u32[]{:S(2)}) collective-permute-start(bf16[4,128,1280]{2,1,0:T(8,128)(2,1)} %bitcast_dynamic-update-slice_fusion.32), channel_id=1, source_target_pairs={{0,4},{4,0},{8,12},{12,8},{16,20},{20,16},{24,28},{28,24},{1,5},{5... | collective-permute-start | bytes 3932168 | tf_op jit(solution)/shard_map/ppermute | solution.py:379
  165.7 100.0 %collective-permute-start.39 = (bf16[256,1024]{1,0:T(8,128)(2,1)}, bf16[256,1024]{1,0:T(8,128)(2,1)}, u32[]{:S(2)}, u32[]{:S(2)}) collective-permute-start(bf16[256,1024]{1,0:T(8,128)(2,1)} %get-tuple-element.128), channel_id=1, source_target_pairs={{0,2},{1,3},{2,0},{3,1},{4,6},{5,7},{6,4},{7,5},{8,10},{9,11},{10,... | collective-permute-start | bytes 1572872 | tf_op jit(solution)/shard_map/ppermute | solution.py:420
  178.6 129.7 %collective-permute-start.25 = (bf16[4,128,768]{2,1,0:T(8,128)(2,1)}, bf16[4,128,768]{2,1,0:T(8,128)(2,1)}, u32[]{:S(2)}, u32[]{:S(2)}) collective-permute-start(bf16[4,128,768]{2,1,0:T(8,128)(2,1)} %constant_dynamic-update-slice_fusion), channel_id=1, source_target_pairs={{0,4},{4,0},{8,12},{12,8},{16,20},{20,16},{24,28},{28,24},{1,5},{5... | collective-permute-start | bytes 2359304 | tf_op jit(solution)/shard_map/ppermute | solution.py:379
  180.2 177.6 %collective-permute-start.35 = (bf16[4,128,1024]{2,1,0:T(8,128)(2,1)}, bf16[4,128,1024]{2,1,0:T(8,128)(2,1)}, u32[]{:S(2)}, u32[]{:S(2)}) collective-permute-start(bf16[4,128,1024]{2,1,0:T(8,128)(2,1)} %bitcast_dynamic-update-slice_fusion.36), channel_id=1, source_target_pairs={{0,4},{4,0},{8,12},{12,8},{16,20},{20,16},{24,28},{28,24},{1,5},{5... | collective-permute-start | bytes 3145736 | tf_op jit(solution)/shard_map/ppermute | solution.py:379
  201.2 88.9 %collective-permute-start.7 = (bf16[2,2,512,256]{3,2,1,0:T(8,128)(2,1)}, bf16[2,2,512,256]{3,2,1,0:T(8,128)(2,1)S(1)}, u32[]{:S(2)}, u32[]{:S(2)}) collective-permute-start(bf16[2,2,512,256]{3,2,1,0:T(8,128)(2,1)} %get-tuple-element.38.own_ref), channel_id=1, source_target_pairs={{0,4},{4,8},{8,12},{12,16},{16,20},{20,24},{24,28},{1,5},{5,9},{9,... | collective-permute-start | bytes 3145736 | tf_op jit(solution)/shard_map/ppermute | solution.py:561
  265.6 97.8 %collective-permute-start.31 = (bf16[4,128,1280]{2,1,0:T(8,128)(2,1)}, bf16[4,128,1280]{2,1,0:T(8,128)(2,1)}, u32[]{:S(2)}, u32[]{:S(2)}) collective-permute-start(bf16[4,128,1280]{2,1,0:T(8,128)(2,1)} %bitcast_dynamic-update-slice_fusion.28), channel_id=1, source_target_pairs={{0,4},{4,0},{8,12},{12,8},{16,20},{20,16},{24,28},{28,24},{1,5},{5... | collective-permute-start | bytes 3932168 | tf_op jit(solution)/shard_map/ppermute | solution.py:379
  387.5 58.5 %collective-permute-start.26 = (bf16[2,2,512,256]{3,2,1,0:T(8,128)(2,1)}, bf16[2,2,512,256]{3,2,1,0:T(8,128)(2,1)}, u32[]{:S(2)}, u32[]{:S(2)}) collective-permute-start(bf16[2,2,512,256]{3,2,1,0:T(8,128)(2,1)} %get-tuple-element.43.own_ref), channel_id=1, source_target_pairs={{0,4},{4,8},{8,12},{12,16},{16,20},{20,24},{24,28},{1,5},{5,9},{9,... | collective-permute-start | bytes 3145736 | tf_op jit(solution)/shard_map/ppermute | solution.py:561
  441.6 69.1 %collective-permute-start.72 = (bf16[512,1024]{1,0:T(8,128)(2,1)}, bf16[512,1024]{1,0:T(8,128)(2,1)}, u32[]{:S(2)}, u32[]{:S(2)}) collective-permute-start(bf16[512,1024]{1,0:T(8,128)(2,1)} %convolution_convert_fusion.2), channel_id=1, source_target_pairs={{0,4},{4,0},{8,12},{12,8},{16,20},{20,16},{24,28},{28,24},{1,5},{5... | collective-permute-start | bytes 3145736 | tf_op jit(solution)/shard_map/ppermute | solution.py:406
  471.6 64.0 %collective-permute-start.41 = (bf16[2,2,512,256]{3,2,1,0:T(8,128)(2,1)}, bf16[2,2,512,256]{3,2,1,0:T(8,128)(2,1)}, u32[]{:S(2)}, u32[]{:S(2)}) collective-permute-start(bf16[2,2,512,256]{3,2,1,0:T(8,128)(2,1)} %get-tuple-element.51), channel_id=1, source_target_pairs={{4,0},{8,4},{12,8},{16,12},{20,16},{24,20},{28,24},{5,1},{9,5},{13... | collective-permute-start | bytes 3145736 | tf_op jit(solution)/shard_map/ppermute | solution.py:582
  472.9 62.7 %collective-permute-start.42 = (bf16[2,512,256]{2,1,0:T(8,128)(2,1)}, bf16[2,512,256]{2,1,0:T(8,128)(2,1)}, u32[]{:S(2)}, u32[]{:S(2)}) collective-permute-start(bf16[2,512,256]{2,1,0:T(8,128)(2,1)} %get-tuple-element.52), channel_id=1, source_target_pairs={{8,0},{12,4},{16,8},{20,12},{24,16},{28,20},{9,1},{13,5},{17,9},{2... | collective-permute-start | bytes 1572872 | tf_op jit(solution)/shard_map/ppermute | solution.py:583
  479.0 76.2 %collective-permute-start.36 = (bf16[2,256,1024]{2,1,0:T(8,128)(2,1)}, bf16[2,256,1024]{2,1,0:T(8,128)(2,1)}, u32[]{:S(2)}, u32[]{:S(2)}) collective-permute-start(bf16[2,256,1024]{2,1,0:T(8,128)(2,1)} %dynamic-slice_bitcast_fusion.2), channel_id=1, source_target_pairs={{0,1},{1,0},{2,3},{3,2},{4,5},{5,4},{6,7},{7,6},{8,9},{9,8},{10,11... | collective-permute-start | bytes 3145736 | tf_op jit(solution)/shard_map/ppermute | solution.py:438
  485.0 73.9 %collective-permute-start.64 = (bf16[512,1280]{1,0:T(8,128)(2,1)}, bf16[512,1280]{1,0:T(8,128)(2,1)}, u32[]{:S(2)}, u32[]{:S(2)}) collective-permute-start(bf16[512,1280]{1,0:T(8,128)(2,1)} %convolution_convert_fusion), channel_id=1, source_target_pairs={{0,4},{4,0},{8,12},{12,8},{16,20},{20,16},{24,28},{28,24},{1,5},{5... | collective-permute-start | bytes 3932168 | tf_op jit(solution)/shard_map/ppermute | solution.py:406
  644.5 56.0 %collective-permute-start.48 = (bf16[2,2,512,256]{3,2,1,0:T(8,128)(2,1)}, bf16[2,2,512,256]{3,2,1,0:T(8,128)(2,1)}, u32[]{:S(2)}, u32[]{:S(2)}) collective-permute-start(bf16[2,2,512,256]{3,2,1,0:T(8,128)(2,1)} %get-tuple-element.58), channel_id=1, source_target_pairs={{4,0},{8,4},{12,8},{16,12},{20,16},{24,20},{28,24},{5,1},{9,5},{13... | collective-permute-start | bytes 3145736 | tf_op jit(solution)/shard_map/ppermute | solution.py:582
  645.8 54.7 %collective-permute-start.49 = (bf16[2,512,256]{2,1,0:T(8,128)(2,1)}, bf16[2,512,256]{2,1,0:T(8,128)(2,1)}, u32[]{:S(2)}, u32[]{:S(2)}) collective-permute-start(bf16[2,512,256]{2,1,0:T(8,128)(2,1)} %get-tuple-element.59), channel_id=1, source_target_pairs={{8,0},{12,4},{16,8},{20,12},{24,16},{28,20},{9,1},{13,5},{17,9},{2... | collective-permute-start | bytes 1572872 | tf_op jit(solution)/shard_map/ppermute | solution.py:583
  682.5 76.5 %collective-permute-start.60 = (bf16[512,1280]{1,0:T(8,128)(2,1)}, bf16[512,1280]{1,0:T(8,128)(2,1)}, u32[]{:S(2)}, u32[]{:S(2)}) collective-permute-start(bf16[512,1280]{1,0:T(8,128)(2,1)} %convolution_convert_fusion.1), channel_id=1, source_target_pairs={{0,4},{4,0},{8,12},{12,8},{16,20},{20,16},{24,28},{28,24},{1,5},{5... | collective-permute-start | bytes 3932168 | tf_op jit(solution)/shard_map/ppermute | solution.py:406
  714.1 100.4 %collective-permute-start.50 = (bf16[2,256,1024]{2,1,0:T(8,128)(2,1)}, bf16[2,256,1024]{2,1,0:T(8,128)(2,1)}, u32[]{:S(2)}, u32[]{:S(2)}) collective-permute-start(bf16[2,256,1024]{2,1,0:T(8,128)(2,1)} %dynamic-slice_bitcast_fusion), channel_id=1, source_target_pairs={{0,1},{1,0},{2,3},{3,2},{4,5},{5,4},{6,7},{7,6},{8,9},{9,8},{10,11... | collective-permute-start | bytes 3145736 | tf_op jit(solution)/shard_map/ppermute | solution.py:438
  717.2 91.8 %collective-permute-start.52 = (bf16[512,768]{1,0:T(8,128)(2,1)S(1)}, bf16[512,768]{1,0:T(8,128)(2,1)S(1)}, u32[]{:S(2)}, u32[]{:S(2)}) collective-permute-start(bf16[512,768]{1,0:T(8,128)(2,1)S(1)} %convolution_convert_fusion.5), channel_id=1, source_target_pairs={{0,4},{4,0},{8,12},{12,8},{16,20},{20,16},{24,28},{28,24},{1,5},{5... | collective-permute-start | bytes 2359304 | tf_op jit(solution)/shard_map/ppermute | solution.py:406
  (153 other events, 2315.5 us)

commit v2 on v1

--- a/solution.py
+++ b/solution.py
@@ -350,6 +350,102 @@
     )(normed, weight, bias)
 
 
+def grad_kernel(side_ref, left_ref, *refs, chunk):
+    rights, mine_ref, sent_ref = refs[:-2], refs[-2], refs[-1]
+    first = side_ref[0] == 0
+    at = 0
+    for right_ref in rights:
+        cols = slice(at, at + right_ref.shape[1])
+        at += right_ref.shape[1]
+        product = dot_tn(left_ref[...], right_ref[...])
+        for pair in range(product.shape[0] // (2 * chunk)):
+            low = product[2 * pair * chunk : (2 * pair + 1) * chunk]
+            high = product[(2 * pair + 1) * chunk : (2 * pair + 2) * chunk]
+            mine_ref[pair, :, cols] = jnp.where(first, low, high).astype(mine_ref.dtype)
+            sent_ref[pair, :, cols] = jnp.where(first, high, low).astype(BF)
+
+
+def grad_call(side, left, rights, chunk):
+    rows, width = left.shape
+    cols = sum(right.shape[1] for right in rights)
+    tile = max(256, 2 * chunk)
+    pairs = tile // (2 * chunk)
+    outer = width // (2 * chunk)
+    out_spec = pl.BlockSpec((pairs, chunk, cols), lambda m, s: (m, 0, 0))
+    return pl.pallas_call(
+        functools.partial(grad_kernel, chunk=chunk),
+        grid_spec=pltpu.PrefetchScalarGridSpec(
+            num_scalar_prefetch=1,
+            grid=(width // tile,),
+            in_specs=[pl.BlockSpec((rows, tile), lambda m, s: (0, m))]
+            + [pl.BlockSpec(right.shape, lambda m, s: (0, 0)) for right in rights],
+            out_specs=[out_spec, out_spec],
+        ),
+        out_shape=[
+            jax.ShapeDtypeStruct((outer, chunk, cols), BF),
+            jax.ShapeDtypeStruct((outer, chunk, cols), BF),
+        ],
+        name="weight_grad",
+    )(side, left, *rights)
+
+
+def pair_kernel(at_ref, mine_ref, came_ref, own_ref, *part_refs):
+    turn = pl.program_id(0)
+    total = mine_ref[0].astype(F32) + came_ref[0].astype(F32)
+
+    @pl.when(turn == 0)
+    def _():
+        own_ref[...] = total
+
+    for index, part_ref in enumerate(part_refs):
+
+        @pl.when(turn == index + 1)
+        def _(part_ref=part_ref):
+            part_ref[...] = total.astype(BF)
+
+
+def pair_call(at, mine, came):
+    outer, chunk, cols = mine.shape
+    in_spec = pl.BlockSpec((1, chunk, cols), lambda d, a: ((a[0] + d) % outer, 0, 0))
+    out_spec = pl.BlockSpec((chunk, cols), lambda d, a: (0, 0))
+    return pl.pallas_call(
+        pair_kernel,
+        grid_spec=pltpu.PrefetchScalarGridSpec(
+            num_scalar_prefetch=1,
+            grid=(outer,),
+            in_specs=[in_spec, in_spec],
+            out_specs=[out_spec] * outer,
+        ),
+        out_shape=[jax.ShapeDtypeStruct((chunk, cols), F32)]
+        + [jax.ShapeDtypeStruct((chunk, cols), BF)] * (outer - 1),
+        name="pair_sum",
+    )(at, mine, came)
+
+
+def place_kernel(me_ref, own_ref, beside_ref, across_ref, diagonal_ref, out_ref):
+    for index, ref in enumerate((own_ref, beside_ref, across_ref, diagonal_ref)):
+
+        @pl.when(pl.program_id(0) == index)
+        def _(ref=ref):
+            out_ref[...] = ref[...]
+
+
+def place_call(me, blocks):
+    rows, width = blocks[0].shape
+    whole = pl.BlockSpec((rows, width), lambda i, m: (0, 0))
+    return pl.pallas_call(
+        place_kernel,
+        grid_spec=pltpu.PrefetchScalarGridSpec(
+            num_scalar_prefetch=1,
+            grid=(4,),
+            in_specs=[whole] * 4,
+            out_specs=pl.BlockSpec((rows, width), lambda i, m: (m[0] ^ i, 0)),
+        ),
+        out_shape=jax.ShapeDtypeStruct((4 * rows, width), blocks[0].dtype),
+        name="place",
+    )(me, *blocks)
+
+
 def flipped(count, bit):
     return [(i, i ^ bit) for i in range(count)]
 
@@ -387,30 +483,16 @@
     return lax.all_gather(piece, "seq", axis=0, tiled=True)
 
 
-def halves(values):
-    count = lax.axis_size("seq")
-    side = lax.axis_index("seq") % 2
-    rows, width = values.shape
-    split = values.reshape(rows, count // 2, 2, width // count)
-    mine = lax.dynamic_index_in_dim(split, side, 2, keepdims=False)
-    other = lax.dynamic_index_in_dim(split, 1 - side, 2, keepdims=False)
-    return mine.reshape(rows, width // 2), other.reshape(rows, width // 2)
-
-
-def scatter_grad(left, right):
+def scatter_grad(left, rights):
     count = lax.axis_size("seq")
     outer = count // 2
-    at = lax.axis_index("seq") // 2
-    mine, other = left
-    sent = dot_tn(other, right).astype(BF)
+    place = lax.axis_index("seq")
+    chunk = left.shape[1] // count
+    mine, sent = grad_call((place % 2)[None], left, rights, chunk)
     came = lax.ppermute(sent, "seq", flipped(count, 1))
-    paired = (dot_tn(mine, right) + came.astype(F32)).astype(BF)
-    line = paired.reshape(outer, -1, right.shape[1])
-    total = lax.dynamic_index_in_dim(line, at, 0, keepdims=False).astype(F32)
-    for distance in range(1, outer):
-        part = lax.dynamic_index_in_dim(line, (at + distance) % outer, 0, keepdims=False)
-        part = lax.ppermute(part, "seq", rolled_outer(outer, distance))
-        total = total + part.astype(F32)
+    total, *parts = pair_call((place // 2)[None], mine, came)
+    for distance, part in enumerate(parts, 1):
+        total = total + lax.ppermute(part, "seq", rolled_outer(outer, distance)).astype(F32)
     return total
 
 
@@ -420,12 +502,7 @@
     across = lax.ppermute(rows, "tensor", flipped(count, 2))
     beside = lax.ppermute(rows, "tensor", flipped(count, 1))
     diagonal = lax.ppermute(across, "tensor", flipped(count, 1))
-    out = jnp.zeros((count,) + rows.shape, rows.dtype)
-    out = lax.dynamic_update_index_in_dim(out, rows, me, 0)
-    out = lax.dynamic_update_index_in_dim(out, beside, me ^ 1, 0)
-    out = lax.dynamic_update_index_in_dim(out, across, me ^ 2, 0)
-    out = lax.dynamic_update_index_in_dim(out, diagonal, me ^ 3, 0)
-    return out.reshape(count * rows.shape[0], rows.shape[1])
+    return place_call(me[None], (rows, beside, across, diagonal))
 
 
 def scatter_tokens(partial):
@@ -574,20 +651,35 @@
         normed_rows, unit, scale_inv, query, own, near, far, hidden, slope, mixed, lse = kept[layer]
         bias_grad = jnp.sum(gradient, axis=0)
         grad_rows = gather_tokens(gradient.astype(BF))
-        grad_halves = halves(grad_rows)
-        normed_halves = halves(normed_rows)
         mixed_grad = dot_nn(grad_rows, fall_full[:, :head_width]).astype(BF)
-        fall_grad = scatter_grad(grad_halves, jnp.concatenate([mixed, hidden], axis=1))
+        whole = WHOLE[layer]
+        if not whole:
+            fall_grad = scatter_grad(grad_rows, (mixed, hidden))
         dq, down, dnear, dfar = bwd_call(counts, query, own, near, far, mixed, mixed_grad, lse, tables)
         came_near = lax.ppermute(dnear, "seq", shifted(seq_count, -1))
         came_far = lax.ppermute(dfar, "seq", shifted(seq_count, -2))
         hidden_grad = dot_nn(grad_rows, fall_full[:, head_width:])
         rise_grad = (hidden_grad * slope).astype(BF)
         rise_bias_grad = jnp.sum(rise_grad, axis=0, dtype=F32)
-        up_grad = scatter_grad(normed_halves, rise_grad)
+        if not whole:
+            up_grad = scatter_grad(normed_rows, (rise_grad,))
         normed_part = dot_nt(rise_grad, up_full)
         joint_grad, joint_bias_grad = join_call(dq, down, came_near, came_far, tables)
-        joint_weight_grad = scatter_grad(normed_halves, joint_grad)
+        if whole:
+            every = jnp.concatenate(
+                [
+                    dot_tn(grad_rows, jnp.concatenate([mixed, hidden], axis=1)).astype(BF),
+                    dot_tn(normed_rows, rise_grad).astype(BF),
+                    dot_tn(normed_rows, joint_grad).astype(BF),
+                ],
+                axis=1,
+            )
+            every = lax.psum_scatter(every, "seq", scatter_dimension=0, tiled=True).astype(F32)
+            fall_grad = every[:, : head_width + hidden_width]
+            up_grad = every[:, head_width + hidden_width : head_width + 2 * hidden_width]
+            joint_weight_grad = every[:, head_width + 2 * hidden_width :]
+        else:
+            joint_weight_grad = scatter_grad(normed_rows, (joint_grad,))
         normed_part = normed_part + dot_nt(joint_grad, qkv_full)
         normed_grad = scatter_tokens(normed_part.astype(BF))
         gain_grad = jnp.sum(normed_grad * unit, axis=0)
@@ -640,7 +732,8 @@
     )
 
 
-GATHER = (gather_rows, gather_rows)
+GATHER = (gather_rows, gather_rows_whole)
+WHOLE = (False, True)
 
 
 def solution(mesh):

time: 858 us -> 732 us (0.85)
  local copies, waits for them, and re-layouts: 203 us -> 63.6 us
  waiting for transfers between devices: 250 us -> 315 us
  starting transfers between devices: 179 us -> 117 us
  Pallas kernels: 89.7 us -> 122 us
  matrix products: 81.6 us -> 55.6 us
  between operations: 3.12 us -> 15.6 us
    dynamic_slice x20 -> x0, local copies, waits for them, and re-layouts: 73.5 us -> none  [the longest x6 34.7 us: halves(): other = lax.dynamic_index_in_dim(split, 1 - side, 2, keepdims=False)]
    ppermute x2, waiting for transfers between devices: 20.6 us -> 91.5 us  [local(): came_far = lax.ppermute(dfar, 'seq', shifted(seq_count, -2))]
    pallas_call x0 -> x10, Pallas kernels: none -> 43.3 us  [the longest x3 18.5 us: grad_call(): pl.pallas_call(functools.partial(grad_kernel, chunk=chunk), grid_spec=plt...]
    ppermute x6 -> x3, waiting for transfers between devices: 43.6 us -> 3.04 us  [scatter_grad(): came = lax.ppermute(sent, 'seq', flipped(count, 1))]
    ppermute x6 -> x3, starting transfers between devices: 42.6 us -> 2.73 us  [scatter_grad(): came = lax.ppermute(sent, 'seq', flipped(count, 1))]
    ppermute x18 -> x9, waiting for transfers between devices: 64.3 us -> 24.5 us  [scatter_grad(): lax.ppermute(part, 'seq', rolled_outer(outer, distance)).astype(F32)]
    all_to_all x2, waiting for transfers between devices: 6.21 us -> 39.5 us  [exchanged(): return lax.all_to_all(rows, ('seq', 'tensor'), 0, 0, tiled=True)]
    ppermute x18 -> x9, starting transfers between devices: 18.4 us -> 50.4 us  [scatter_grad(): lax.ppermute(part, 'seq', rolled_outer(outer, distance)).astype(F32)]
  transfers between devices with their start and end apart: 78 -> 58, of which waited for: 21 -> 26; matrix products, arithmetic and copies ran while one was open for 35% -> 18% of each run, Pallas kernels for 8% -> 13%
where the time goes in v2:
time: 732 us; the launch traced here: 730 us
  waiting for transfers between devices  315 us (43%)
  Pallas kernels  122 us (17%)
  starting transfers between devices  117 us (16%)
  local copies, waits for them, and re-layouts  63.6 us (9%)
  matrix products  55.6 us (8%)
  other arithmetic  40.9 us (6%)
  between operations  15.6 us (2%)
    ppermute x2, waiting for transfers between devices, local(): came_far = lax.ppermute(dfar, 'seq', shifted(seq_count, -2))  91.5 us
    ppermute x9, starting transfers between devices, scatter_grad(): lax.ppermute(part, 'seq', rolled_outer(outer, distance)).astype(F32)  50.4 us
    ppermute x4, waiting for transfers between devices, gather_tokens(): across = lax.ppermute(rows, 'tensor', flipped(count, 2))  41 us
    all_to_all x2, waiting for transfers between devices, exchanged(): return lax.all_to_all(rows, ('seq', 'tensor'), 0, 0, tiled=True)  39.5 us
    ppermute x3, waiting for transfers between devices, gather_rows(): other = lax.ppermute(line, 'seq', flipped(count, 1))  39.3 us
    ppermute x4, waiting for transfers between devices, scatter_tokens(): across = lax.ppermute(far.astype(BF), 'tensor', flipped(count, 2))  32 us
    ppermute x9, waiting for transfers between devices, scatter_grad(): lax.ppermute(part, 'seq', rolled_outer(outer, distance)).astype(F32)  24.5 us
    pallas_call x2, Pallas kernels, bwd_call(): pl.pallas_call(bwd_kernel, grid_spec=pltpu.PrefetchScalarGridSpec(num_sca...  24.4 us
  transfers between devices with their start and end apart: 58, of which 26 were waited for; matrix products, arithmetic and copies ran while one was open for 18% of the time, Pallas kernels for 13%

profile of v2, /device:TPU:0, one launch (start us, length us, event | category | flops | bytes accessed | tf_op | source)
XLA Modules:
  0.0 729.5 jit_solution(68911472818220646)
XLA Ops:
  37.5 34.5 %all-to-all-done = bf16[32,2,320]{2,1,0:T(2,128)(2,1)S(1)} async-done(((bf16[32,2,320]{2,1,0:T(2,128)(2,1)}), bf16[32,2,320]{2,1,0:T(2,128)(2,1)S(1)}, u32[]{:S(2)}, u32[]{:S(2)}) %all-to-all-start) | async-done | bytes 40992 | tf_op jit(solution)/shard_map/all_to_all | solution.py:525
  88.5 10.3 %collective-permute-done.13 = bf16[128,1024]{1,0:T(8,128)(2,1)} collective-permute-done((bf16[128,1024]{1,0:T(8,128)(2,1)S(1)}, bf16[128,1024]{1,0:T(8,128)(2,1)}, u32[]{:S(2)}, u32[]{:S(2)}) %collective-permute-start.13) | collective-permute-done | bytes 262176 | tf_op jit(solution)/shard_map/ppermute | solution.py:473
  105.1 8.2 %collective-permute-done.14 = bf16[128,1024]{1,0:T(8,128)(2,1)} collective-permute-done((bf16[128,1024]{1,0:T(8,128)(2,1)S(1)}, bf16[128,1024]{1,0:T(8,128)(2,1)}, u32[]{:S(2)}, u32[]{:S(2)}) %collective-permute-start.14) | collective-permute-done | bytes 262176 | tf_op jit(solution)/shard_map/ppermute | solution.py:473
  123.7 8.2 %collective-permute-done.1.across_ref = bf16[256,1024]{1,0:T(8,128)(2,1)S(1)} collective-permute-done((bf16[256,1024]{1,0:T(8,128)(2,1)}, bf16[256,1024]{1,0:T(8,128)(2,1)S(1)}, u32[]{:S(2)}, u32[]{:S(2)}) %collective-permute-start.1) | collective-permute-done | bytes 524320 | tf_op jit(solution)/shard_map/ppermute | solution.py:502
  133.6 19.8 %collective-permute-done.6 = bf16[4,128,768]{2,1,0:T(8,128)(2,1)S(1)} collective-permute-done((bf16[4,128,768]{2,1,0:T(8,128)(2,1)}, bf16[4,128,768]{2,1,0:T(8,128)(2,1)S(1)}, u32[]{:S(2)}, u32[]{:S(2)}) %collective-permute-start.6) | collective-permute-done | bytes 786464 | tf_op jit(solution)/shard_map/ppermute | solution.py:475
  178.6 7.8 %up.2 = (bf16[1024,1024]{1,0:T(8,128)(2,1)}, f32[1024,1024]{1,0:T(8,128)}) custom-call(bf16[1024,1024]{1,0:T(8,128)(2,1)} %place.4.x_ref.left_ref, bf16[1024,1024]{1,0:T(8,128)(2,1)} %bitcast.186, f32[1,1024]{1,0:T(1,128)} %squeeze.72.b_ref), custom_call_target="tpu_custom_call" | custom-call | tf_op jit(solution)/shard_map/up/pallas_call | solution.py:336
  186.4 16.6 %collective-permute-done.12 = bf16[4,128,1280]{2,1,0:T(8,128)(2,1)} collective-permute-done((bf16[4,128,1280]{2,1,0:T(8,128)(2,1)}, bf16[4,128,1280]{2,1,0:T(8,128)(2,1)}, u32[]{:S(2)}, u32[]{:S(2)}) %collective-permute-start.12) | collective-permute-done | bytes 1310752 | tf_op jit(solution)/shard_map/ppermute | solution.py:475
  205.5 17.8 %collective-permute-done.7.near_ref = bf16[2,2,512,256]{3,2,1,0:T(8,128)(2,1)} collective-permute-done((bf16[2,2,512,256]{3,2,1,0:T(8,128)(2,1)}, bf16[2,2,512,256]{3,2,1,0:T(8,128)(2,1)}, u32[]{:S(2)}, u32[]{:S(2)}) %collective-permute-start.7) | collective-permute-done | bytes 1048608 | tf_op jit(solution)/shard_map/ppermute | solution.py:638
  223.3 7.7 %attend.2 = (bf16[1024,256]{1,0:T(8,128)(2,1)}, f32[2,2,1024]{2,1,0:T(2,128)}) custom-call(s32[2]{0:T(128)} %fusion.29.n_ref, bf16[1024,256]{1,0:T(8,128)(2,1)} %get-tuple-element.55.q_ref, bf16[2,2,512,256]{3,2,1,0:T(8,128)(2,1)} %get-tuple-element.56.own_ref, bf16[2,2,512,256]{3,2,1,0:T(8,128)(2,1)} %collective-permute-done.7.near_ref, ...), custom_call_target="tpu_custom_call" | custom-call | tf_op jit(solution)/shard_map/attend/pallas_call | solution.py:161
  244.3 12.3 %collective-permute-done.18 = bf16[256,1024]{1,0:T(8,128)(2,1)} collective-permute-done((bf16[256,1024]{1,0:T(8,128)(2,1)}, bf16[256,1024]{1,0:T(8,128)(2,1)}, u32[]{:S(2)}, u32[]{:S(2)}) %collective-permute-start.18) | collective-permute-done | bytes 524320 | tf_op jit(solution)/shard_map/ppermute | solution.py:518
  262.1 11.6 %collective-permute-done.20.across_ref = bf16[256,1024]{1,0:T(8,128)(2,1)S(1)} collective-permute-done((bf16[256,1024]{1,0:T(8,128)(2,1)S(1)}, bf16[256,1024]{1,0:T(8,128)(2,1)S(1)}, u32[]{:S(2)}, u32[]{:S(2)}) %collective-permute-start.20) | collective-permute-done | bytes 524320 | tf_op jit(solution)/shard_map/ppermute | solution.py:502
  274.2 9.1 %collective-permute-done.27.across_ref = bf16[256,1024]{1,0:T(8,128)(2,1)} collective-permute-done((bf16[256,1024]{1,0:T(8,128)(2,1)}, bf16[256,1024]{1,0:T(8,128)(2,1)}, u32[]{:S(2)}, u32[]{:S(2)}) %collective-permute-start.27) | collective-permute-done | bytes 524320 | tf_op jit(solution)/shard_map/ppermute | solution.py:502
  315.0 7.8 %up.3 = (bf16[1024,1024]{1,0:T(8,128)(2,1)}, f32[1024,1024]{1,0:T(8,128)}) custom-call(bf16[1024,1024]{1,0:T(8,128)(2,1)} %place.5.x_ref, bf16[1024,1024]{1,0:T(8,128)(2,1)} %bitcast.195, f32[1,1024]{1,0:T(1,128)} %squeeze.78.b_ref), custom_call_target="tpu_custom_call" | custom-call | tf_op jit(solution)/shard_map/up/pallas_call | solution.py:336
  338.6 12.3 %attend_back.2 = (bf16[1024,256]{1,0:T(8,128)(2,1)}, f32[2,2,512,256]{3,2,1,0:T(8,128)}, bf16[2,2,512,256]{3,2,1,0:T(8,128)(2,1)}, bf16[2,512,256]{2,1,0:T(8,128)(2,1)}) custom-call(s32[2]{0:T(128)} %fusion.29.n_ref, bf16[1024,256]{1,0:T(8,128)(2,1)} %get-tuple-element.60.q_ref, bf16[2,2,512,256]{3,2,1,0:T(8,128)(2,1)} %get-tuple-element.61.own_ref, ...), custom_call_target="tpu_custom_call" | custom-call | tf_op jit(solution)/shard_map/attend_back/pallas_call | solution.py:244
  364.1 44.4 %collective-permute-done.30.far_ref = bf16[2,512,256]{2,1,0:T(8,128)(2,1)S(1)} collective-permute-done((bf16[2,512,256]{2,1,0:T(8,128)(2,1)S(1)}, bf16[2,512,256]{2,1,0:T(8,128)(2,1)S(1)}, u32[]{:S(2)}, u32[]{:S(2)}) %collective-permute-start.30) | collective-permute-done | bytes 524320 | tf_op jit(solution)/shard_map/ppermute | solution.py:660
  443.5 10.2 %collective-permute-done.32 = bf16[256,1024]{1,0:T(8,128)(2,1)} collective-permute-done((bf16[256,1024]{1,0:T(8,128)(2,1)}, bf16[256,1024]{1,0:T(8,128)(2,1)}, u32[]{:S(2)}, u32[]{:S(2)}) %collective-permute-start.32) | collective-permute-done | bytes 524320 | tf_op jit(solution)/shard_map/ppermute | solution.py:518
  455.8 8.6 %collective-permute-done.25 = bf16[256,1024]{1,0:T(8,128)(2,1)S(1)} collective-permute-done((bf16[256,1024]{1,0:T(8,128)(2,1)S(1)}, bf16[256,1024]{1,0:T(8,128)(2,1)S(1)}, u32[]{:S(2)}, u32[]{:S(2)}) %collective-permute-start.25) | collective-permute-done | bytes 524320 | tf_op jit(solution)/shard_map/ppermute | solution.py:518
  468.8 12.1 %collective-permute-done.34.across_ref = bf16[256,1024]{1,0:T(8,128)(2,1)S(1)} collective-permute-done((bf16[256,1024]{1,0:T(8,128)(2,1)S(1)}, bf16[256,1024]{1,0:T(8,128)(2,1)S(1)}, u32[]{:S(2)}, u32[]{:S(2)}) %collective-permute-start.34) | collective-permute-done | bytes 524320 | tf_op jit(solution)/shard_map/ppermute | solution.py:502
  489.7 12.1 %attend_back.3 = (bf16[1024,256]{1,0:T(8,128)(2,1)}, f32[2,2,512,256]{3,2,1,0:T(8,128)}, bf16[2,2,512,256]{3,2,1,0:T(8,128)(2,1)}, bf16[2,512,256]{2,1,0:T(8,128)(2,1)}) custom-call(s32[2]{0:T(128)} %fusion.29.n_ref, bf16[1024,256]{1,0:T(8,128)(2,1)} %get-tuple-element.55.q_ref, bf16[2,2,512,256]{3,2,1,0:T(8,128)(2,1)} %get-tuple-element.56.own_ref, ...), custom_call_target="tpu_custom_call" | custom-call | tf_op jit(solution)/shard_map/attend_back/pallas_call | solution.py:244
  529.0 47.1 %collective-permute-done.37.far_ref = bf16[2,512,256]{2,1,0:T(8,128)(2,1)} collective-permute-done((bf16[2,512,256]{2,1,0:T(8,128)(2,1)}, bf16[2,512,256]{2,1,0:T(8,128)(2,1)}, u32[]{:S(2)}, u32[]{:S(2)}) %collective-permute-start.37) | collective-permute-done | bytes 524320 | tf_op jit(solution)/shard_map/ppermute | solution.py:660
  602.7 15.9 %collective-permute-start.51 = (bf16[128,1024]{1,0:T(8,128)(2,1)}, bf16[128,1024]{1,0:T(8,128)(2,1)}, u32[]{:S(2)}, u32[]{:S(2)}) collective-permute-start(bf16[128,1024]{1,0:T(8,128)(2,1)} %get-tuple-element.98), channel_id=1, source_target_pairs={{0,24},{4,28},{8,0},{12,4},{16,8},{20,12},{24,16},{28,20},{1,25},{... | collective-permute-start | bytes 786440 | tf_op jit(solution)/shard_map/ppermute | solution.py:495
  618.6 10.0 %collective-permute-start.50 = (bf16[128,1024]{1,0:T(8,128)(2,1)}, bf16[128,1024]{1,0:T(8,128)(2,1)}, u32[]{:S(2)}, u32[]{:S(2)}) collective-permute-start(bf16[128,1024]{1,0:T(8,128)(2,1)} %get-tuple-element.97), channel_id=1, source_target_pairs={{0,16},{4,20},{8,24},{12,28},{16,0},{20,4},{24,8},{28,12},{1,17},{... | collective-permute-start | bytes 786440 | tf_op jit(solution)/shard_map/ppermute | solution.py:495
  640.2 14.8 %collective-permute-done.50 = bf16[128,1024]{1,0:T(8,128)(2,1)} collective-permute-done((bf16[128,1024]{1,0:T(8,128)(2,1)}, bf16[128,1024]{1,0:T(8,128)(2,1)}, u32[]{:S(2)}, u32[]{:S(2)}) %collective-permute-start.50) | collective-permute-done | bytes 262176 | tf_op jit(solution)/shard_map/ppermute | solution.py:495
  667.4 15.4 %collective-permute-start.41 = (bf16[128,768]{1,0:T(8,128)(2,1)}, bf16[128,768]{1,0:T(8,128)(2,1)S(1)}, u32[]{:S(2)}, u32[]{:S(2)}) collective-permute-start(bf16[128,768]{1,0:T(8,128)(2,1)} %get-tuple-element.84), channel_id=1, source_target_pairs={{0,8},{4,12},{8,16},{12,20},{16,24},{20,28},{24,0},{28,4},{1,9},{5... | collective-permute-start | bytes 589832 | tf_op jit(solution)/shard_map/ppermute | solution.py:495
  (428 shorter events, 339.2 us)
Async XLA Ops:
  7.2 280.3 %all-gather.5.cloned.1.call-start = ((), (), s32[]{:S(2)}) async-start(), calls=%async_computation.3 | async-start | bytes 1769472 | tf_op jit(solution)/shard_map/all_gather | solution.py:483
  9.6 66.2 %collective-permute-start.3 = (bf16[128,768]{0,1:T(8,128)(2,1)S(1)}, bf16[128,768]{0,1:T(8,128)(2,1)}, u32[]{:S(2)}, u32[]{:S(2)}) collective-permute-start(bf16[128,768]{0,1:T(8,128)(2,1)S(1)} %bitcast.207), channel_id=1, source_target_pairs={{0,8},{4,12},{8,16},{12,20},{16,24},{20,28},{24,0},{28,4},{1,9},{5... | collective-permute-start | bytes 589832 | tf_op jit(solution)/shard_map/ppermute | solution.py:473
  12.7 67.1 %collective-permute-start.4 = (bf16[128,768]{0,1:T(8,128)(2,1)S(1)}, bf16[128,768]{0,1:T(8,128)(2,1)}, u32[]{:S(2)}, u32[]{:S(2)}) collective-permute-start(bf16[128,768]{0,1:T(8,128)(2,1)S(1)} %bitcast.208), channel_id=1, source_target_pairs={{0,16},{4,20},{8,24},{12,28},{16,0},{20,4},{24,8},{28,12},{1,17},{... | collective-permute-start | bytes 589832 | tf_op jit(solution)/shard_map/ppermute | solution.py:473
  15.3 65.6 %collective-permute-start.5 = (bf16[128,768]{0,1:T(8,128)(2,1)S(1)}, bf16[128,768]{0,1:T(8,128)(2,1)}, u32[]{:S(2)}, u32[]{:S(2)}) collective-permute-start(bf16[128,768]{0,1:T(8,128)(2,1)S(1)} %bitcast.209), channel_id=1, source_target_pairs={{0,24},{4,28},{8,0},{12,4},{16,8},{20,12},{24,16},{28,20},{1,25},{... | collective-permute-start | bytes 589832 | tf_op jit(solution)/shard_map/ppermute | solution.py:473
  16.8 102.7 %collective-permute-start.9 = (bf16[128,1280]{1,0:T(8,128)(2,1)S(1)}, bf16[128,1280]{1,0:T(8,128)(2,1)S(1)}, u32[]{:S(2)}, u32[]{:S(2)}) collective-permute-start(bf16[128,1280]{1,0:T(8,128)(2,1)S(1)} %pad_maximum_fusion.4), channel_id=1, source_target_pairs={{0,8},{4,12},{8,16},{12,20},{16,24},{20,28},{24,0},{28,4},{1,9},{5... | collective-permute-start | bytes 983048 | tf_op jit(solution)/shard_map/ppermute | solution.py:473
  17.5 102.7 %collective-permute-start.10 = (bf16[128,1280]{1,0:T(8,128)(2,1)S(1)}, bf16[128,1280]{1,0:T(8,128)(2,1)S(1)}, u32[]{:S(2)}, u32[]{:S(2)}) collective-permute-start(bf16[128,1280]{1,0:T(8,128)(2,1)S(1)} %pad_maximum_fusion.4), channel_id=1, source_target_pairs={{0,16},{4,20},{8,24},{12,28},{16,0},{20,4},{24,8},{28,12},{1,17},{... | collective-permute-start | bytes 983048 | tf_op jit(solution)/shard_map/ppermute | solution.py:473
  20.5 51.5 %all-to-all-start = ((bf16[32,2,320]{2,1,0:T(2,128)(2,1)}), bf16[32,2,320]{2,1,0:T(2,128)(2,1)S(1)}, u32[]{:S(2)}, u32[]{:S(2)}) async-start(bf16[32,2,320]{2,1,0:T(2,128)(2,1)} %reshape.444), calls=%async_computation | async-start | bytes 98304 | tf_op jit(solution)/shard_map/all_to_all | solution.py:525
  26.2 278.8 %all-gather.7.cloned.1.call-start = ((), (), s32[]{:S(2)}) async-start(), calls=%async_computation.4 | async-start | bytes 2949120 | tf_op jit(solution)/shard_map/all_gather | solution.py:483
  27.0 288.0 %all-gather.9.cloned.1.call-start = ((), (), s32[]{:S(2)}) async-start(), calls=%async_computation.6 | async-start | bytes 2359296 | tf_op jit(solution)/shard_map/all_gather | solution.py:483
  75.8 47.1 %collective-permute-start.11 = (bf16[128,1280]{1,0:T(8,128)(2,1)S(1)}, bf16[128,1280]{1,0:T(8,128)(2,1)S(1)}, u32[]{:S(2)}, u32[]{:S(2)}) collective-permute-start(bf16[128,1280]{1,0:T(8,128)(2,1)S(1)} %pad_maximum_fusion.4), channel_id=1, source_target_pairs={{0,24},{4,28},{8,0},{12,4},{16,8},{20,12},{24,16},{28,20},{1,25},{... | collective-permute-start | bytes 983048 | tf_op jit(solution)/shard_map/ppermute | solution.py:473
  113.3 41.0 %collective-permute-start = (bf16[256,1024]{1,0:T(8,128)(2,1)}, bf16[256,1024]{1,0:T(8,128)(2,1)}, u32[]{:S(2)}, u32[]{:S(2)}) collective-permute-start(bf16[256,1024]{1,0:T(8,128)(2,1)} %add_convert_fusion.5.own_ref), channel_id=1, source_target_pairs={{0,1},{1,0},{2,3},{3,2},{4,5},{5,4},{6,7},{7,6},{8,9},{9,8},{10,11... | collective-permute-start | bytes 1572872 | tf_op jit(solution)/shard_map/ppermute | solution.py:503
  120.2 55.7 %collective-permute-start.16 = (bf16[4,128,1024]{2,1,0:T(8,128)(2,1)}, bf16[4,128,1024]{2,1,0:T(8,128)(2,1)}, u32[]{:S(2)}, u32[]{:S(2)}) collective-permute-start(bf16[4,128,1024]{2,1,0:T(8,128)(2,1)} %bitcast_dynamic-update-slice_fusion.10), channel_id=1, source_target_pairs={{0,4},{4,0},{8,12},{12,8},{16,20},{20,16},{24,28},{28,24},{1,5},{5... | collective-permute-start | bytes 3145736 | tf_op jit(solution)/shard_map/ppermute | solution.py:475
  123.7 79.3 %collective-permute-start.12 = (bf16[4,128,1280]{2,1,0:T(8,128)(2,1)}, bf16[4,128,1280]{2,1,0:T(8,128)(2,1)}, u32[]{:S(2)}, u32[]{:S(2)}) collective-permute-start(bf16[4,128,1280]{2,1,0:T(8,128)(2,1)} %bitcast_dynamic-update-slice_fusion.6), channel_id=1, source_target_pairs={{0,4},{4,0},{8,12},{12,8},{16,20},{20,16},{24,28},{28,24},{1,5},{5... | collective-permute-start | bytes 3932168 | tf_op jit(solution)/shard_map/ppermute | solution.py:475
  164.7 58.6 %collective-permute-start.7 = (bf16[2,2,512,256]{3,2,1,0:T(8,128)(2,1)}, bf16[2,2,512,256]{3,2,1,0:T(8,128)(2,1)}, u32[]{:S(2)}, u32[]{:S(2)}) collective-permute-start(bf16[2,2,512,256]{3,2,1,0:T(8,128)(2,1)} %get-tuple-element.56.own_ref), channel_id=1, source_target_pairs={{0,4},{4,8},{8,12},{12,16},{16,20},{20,24},{24,28},{1,5},{5,9},{9,... | collective-permute-start | bytes 3145736 | tf_op jit(solution)/shard_map/ppermute | solution.py:638
  237.3 479.7 %reduce-scatter.2.cloned.1.call-start = ((), (), s32[]{:S(2)}) async-start(), calls=%async_computation.5 | async-start | bytes 7077888 | tf_op jit(solution)/shard_map/reduce_scatter | solution.py:677
  350.9 57.6 %collective-permute-start.29 = (bf16[2,2,512,256]{3,2,1,0:T(8,128)(2,1)}, bf16[2,2,512,256]{3,2,1,0:T(8,128)(2,1)}, u32[]{:S(2)}, u32[]{:S(2)}) collective-permute-start(bf16[2,2,512,256]{3,2,1,0:T(8,128)(2,1)} %get-tuple-element.69), channel_id=1, source_target_pairs={{4,0},{8,4},{12,8},{16,12},{20,16},{24,20},{28,24},{5,1},{9,5},{13... | collective-permute-start | bytes 3145736 | tf_op jit(solution)/shard_map/ppermute | solution.py:659
  358.3 50.2 %collective-permute-start.30 = (bf16[2,512,256]{2,1,0:T(8,128)(2,1)S(1)}, bf16[2,512,256]{2,1,0:T(8,128)(2,1)S(1)}, u32[]{:S(2)}, u32[]{:S(2)}) collective-permute-start(bf16[2,512,256]{2,1,0:T(8,128)(2,1)S(1)} %copy-done.57), channel_id=1, source_target_pairs={{8,0},{12,4},{16,8},{20,12},{24,16},{28,20},{9,1},{13,5},{17,9},{2... | collective-permute-start | bytes 1572872 | tf_op jit(solution)/shard_map/ppermute | solution.py:660
  501.8 74.4 %collective-permute-start.36 = (bf16[2,2,512,256]{3,2,1,0:T(8,128)(2,1)}, bf16[2,2,512,256]{3,2,1,0:T(8,128)(2,1)}, u32[]{:S(2)}, u32[]{:S(2)}) collective-permute-start(bf16[2,2,512,256]{3,2,1,0:T(8,128)(2,1)} %get-tuple-element.76), channel_id=1, source_target_pairs={{4,0},{8,4},{12,8},{16,12},{20,16},{24,20},{28,24},{5,1},{9,5},{13... | collective-permute-start | bytes 3145736 | tf_op jit(solution)/shard_map/ppermute | solution.py:659
  504.8 71.3 %collective-permute-start.37 = (bf16[2,512,256]{2,1,0:T(8,128)(2,1)}, bf16[2,512,256]{2,1,0:T(8,128)(2,1)}, u32[]{:S(2)}, u32[]{:S(2)}) collective-permute-start(bf16[2,512,256]{2,1,0:T(8,128)(2,1)} %get-tuple-element.77), channel_id=1, source_target_pairs={{8,0},{12,4},{16,8},{20,12},{24,16},{28,20},{9,1},{13,5},{17,9},{2... | collective-permute-start | bytes 1572872 | tf_op jit(solution)/shard_map/ppermute | solution.py:660
  513.0 115.5 %collective-permute-start.44 = (bf16[4,128,1280]{2,1,0:T(8,128)(2,1)}, bf16[4,128,1280]{2,1,0:T(8,128)(2,1)S(1)}, u32[]{:S(2)}, u32[]{:S(2)}) collective-permute-start(bf16[4,128,1280]{2,1,0:T(8,128)(2,1)} %get-tuple-element.88), channel_id=1, source_target_pairs={{0,4},{4,0},{8,12},{12,8},{16,20},{20,16},{24,28},{28,24},{1,5},{5... | collective-permute-start | bytes 3932168 | tf_op jit(solution)/shard_map/ppermute | solution.py:492
  529.0 70.2 %collective-permute-start.48 = (bf16[4,128,1024]{2,1,0:T(8,128)(2,1)}, bf16[4,128,1024]{2,1,0:T(8,128)(2,1)}, u32[]{:S(2)}, u32[]{:S(2)}) collective-permute-start(bf16[4,128,1024]{2,1,0:T(8,128)(2,1)} %get-tuple-element.94), channel_id=1, source_target_pairs={{0,4},{4,0},{8,12},{12,8},{16,20},{20,16},{24,28},{28,24},{1,5},{5... | collective-permute-start | bytes 3145736 | tf_op jit(solution)/shard_map/ppermute | solution.py:492
  590.2 73.5 %collective-permute-start.38 = (bf16[2,256,1024]{2,1,0:T(8,128)(2,1)}, bf16[2,256,1024]{2,1,0:T(8,128)(2,1)}, u32[]{:S(2)}, u32[]{:S(2)}) collective-permute-start(bf16[2,256,1024]{2,1,0:T(8,128)(2,1)} %dynamic-slice_bitcast_fusion), channel_id=1, source_target_pairs={{0,1},{1,0},{2,3},{3,2},{4,5},{5,4},{6,7},{7,6},{8,9},{9,8},{10,11... | collective-permute-start | bytes 3145736 | tf_op jit(solution)/shard_map/ppermute | solution.py:515
  596.0 61.7 %collective-permute-start.40 = (bf16[4,128,768]{2,1,0:T(8,128)(2,1)}, bf16[4,128,768]{2,1,0:T(8,128)(2,1)}, u32[]{:S(2)}, u32[]{:S(2)}) collective-permute-start(bf16[4,128,768]{2,1,0:T(8,128)(2,1)} %get-tuple-element.82), channel_id=1, source_target_pairs={{0,4},{4,0},{8,12},{12,8},{16,20},{20,16},{24,28},{28,24},{1,5},{5... | collective-permute-start | bytes 2359304 | tf_op jit(solution)/shard_map/ppermute | solution.py:492
  618.6 36.4 %collective-permute-start.50 = (bf16[128,1024]{1,0:T(8,128)(2,1)}, bf16[128,1024]{1,0:T(8,128)(2,1)}, u32[]{:S(2)}, u32[]{:S(2)}) collective-permute-start(bf16[128,1024]{1,0:T(8,128)(2,1)} %get-tuple-element.97), channel_id=1, source_target_pairs={{0,16},{4,20},{8,24},{12,28},{16,0},{20,4},{24,8},{28,12},{1,17},{... | collective-permute-start | bytes 786440 | tf_op jit(solution)/shard_map/ppermute | solution.py:495
  (95 other events, 1428.0 us)
Sparse Core Ops, SparseCore 0:
  10.2 63.6 all-gather.4
  76.1 82.6 all-gather.6
  237.4 66.9 all-gather.8
  421.8 170.7 reduce-scatter.1

commit v3 on v2

--- a/solution.py
+++ b/solution.py
@@ -446,6 +446,63 @@
     )(me, *blocks)
 
 
+def place_norm_kernel(me_ref, gain_ref, shift_ref, own_ref, beside_ref, across_ref, diagonal_ref, out_ref):
+    for index, ref in enumerate((own_ref, beside_ref, across_ref, diagonal_ref)):
+
+        @pl.when(pl.program_id(0) == index)
+        def _(ref=ref):
+            out_ref[...] = (ref[...].astype(F32) * gain_ref[...] + shift_ref[...]).astype(out_ref.dtype)
+
+
+def place_norm_call(me, gain, shift, blocks):
+    rows, width = blocks[0].shape
+    whole = pl.BlockSpec((rows, width), lambda i, m: (0, 0))
+    line = pl.BlockSpec((1, width), lambda i, m: (0, 0))
+    return pl.pallas_call(
+        place_norm_kernel,
+        grid_spec=pltpu.PrefetchScalarGridSpec(
+            num_scalar_prefetch=1,
+            grid=(4,),
+            in_specs=[line] * 2 + [whole] * 4,
+            out_specs=pl.BlockSpec((rows, width), lambda i, m: (m[0] ^ i, 0)),
+        ),
+        out_shape=jax.ShapeDtypeStruct((4 * rows, width), blocks[0].dtype),
+        name="place_norm",
+    )(me, gain, shift, *blocks)
+
+
+def place_sides_kernel(where_ref, *refs):
+    outer = (len(refs) - 1) // 2
+    mine, other, out_ref = refs[:outer], refs[outer:-1], refs[-1]
+    low = where_ref[1] == 0
+    for index in range(outer):
+
+        @pl.when(pl.program_id(0) == index)
+        def _(index=index):
+            out_ref[0, 0] = jnp.where(low, mine[index][...], other[index][...])
+            out_ref[0, 1] = jnp.where(low, other[index][...], mine[index][...])
+
+
+def place_sides_call(at, side, mine, other):
+    outer = len(mine)
+    chunk, cols = mine[0].shape
+    spec = pl.BlockSpec((chunk, cols), lambda i, w: (0, 0))
+    full = pl.pallas_call(
+        place_sides_kernel,
+        grid_spec=pltpu.PrefetchScalarGridSpec(
+            num_scalar_prefetch=1,
+            grid=(outer,),
+            in_specs=[spec] * (2 * outer),
+            out_specs=pl.BlockSpec(
+                (1, 2, chunk, cols), lambda i, w: (jnp.where(w[0] < i, w[0] - i + outer, w[0] - i), 0, 0, 0)
+            ),
+        ),
+        out_shape=jax.ShapeDtypeStruct((outer, 2, chunk, cols), mine[0].dtype),
+        name="place_sides",
+    )(jnp.stack([at, side]), *mine, *other)
+    return full.reshape(2 * outer * chunk, cols)
+
+
 def flipped(count, bit):
     return [(i, i ^ bit) for i in range(count)]
 
@@ -461,22 +518,22 @@
     ]
 
 
-def gather_rows(piece):
+def gather_line(piece):
+    outer = lax.axis_size("seq") // 2
+    came = [lax.ppermute(piece, "seq", rolled_outer(outer, distance)) for distance in range(1, outer)]
+    return [piece] + came
+
+
+def other_sides(line):
     count = lax.axis_size("seq")
-    outer = count // 2
+    return [lax.ppermute(shard, "seq", flipped(count, 1)) for shard in line]
+
+
+def placed(line, other, after=None):
     place = lax.axis_index("seq")
-    at, side = place // 2, place % 2
-    chunk, cols = piece.shape
-    line = jnp.zeros((outer, chunk, cols), piece.dtype)
-    line = lax.dynamic_update_index_in_dim(line, piece, at, 0)
-    for distance in range(1, outer):
-        came = lax.ppermute(piece, "seq", rolled_outer(outer, distance))
-        line = lax.dynamic_update_index_in_dim(line, came, (at - distance) % outer, 0)
-    other = lax.ppermute(line, "seq", flipped(count, 1))
-    full = jnp.zeros((outer, 2, chunk, cols), piece.dtype)
-    full = lax.dynamic_update_index_in_dim(full, line, side, 1)
-    full = lax.dynamic_update_index_in_dim(full, other, 1 - side, 1)
-    return full.reshape(count * chunk, cols)
+    if after is not None:
+        place, _ = lax.optimization_barrier((place, after))
+    return place_sides_call(place // 2, place % 2, line, other)
 
 
 def gather_rows_whole(piece):
@@ -496,12 +553,14 @@
     return total
 
 
-def gather_tokens(rows):
+def gather_tokens(rows, gain=None, shift=None):
     count = lax.axis_size("tensor")
     me = lax.axis_index("tensor")
     across = lax.ppermute(rows, "tensor", flipped(count, 2))
     beside = lax.ppermute(rows, "tensor", flipped(count, 1))
     diagonal = lax.ppermute(across, "tensor", flipped(count, 1))
+    if gain is not None:
+        return place_norm_call(me[None], gain, shift, (rows, beside, across, diagonal))
     return place_call(me[None], (rows, beside, across, diagonal))
 
 
@@ -617,30 +676,50 @@
     rise_bias = over_seq(parts[4]).reshape(seq_count, layers, groups, -1)
     rise_bias = jnp.transpose(rise_bias, (1, 2, 0, 3)).reshape(layers, 1, hidden_width).astype(F32)
 
-    weights = []
-    for layer in range(layers):
-        gather = GATHER[layer]
-        weights.append(
-            (
-                gather(qkv_weight[layer].reshape(chunk, 3 * head_width)),
-                gather(up_weight[layer]),
-                gather(jnp.concatenate([out_weight[layer], down_weight[layer]], axis=1)),
-            )
+    pieces = [
+        (
+            qkv_weight[layer].reshape(chunk, 3 * head_width),
+            up_weight[layer],
+            jnp.concatenate([out_weight[layer], down_weight[layer]], axis=1),
         )
+        for layer in range(layers)
+    ]
+    lines, arrived = [], ()
+    for piece in pieces[0]:
+        if arrived:
+            piece, _ = lax.optimization_barrier((piece, arrived))
+        lines.append(gather_line(piece))
+        arrived = lines[-1][1:]
+    weights = [tuple(placed(line, other_sides(line)) for line in lines)]
+    others = None
 
     kept = []
     current = block_input
     for layer in range(layers):
+        gain, shift = gains[layer][None], shifts[layer][None]
+        normed, unit, scale_inv = layer_norm(current, gain, shift)
+        if layer == 0:
+            normed_rows = gather_tokens(unit.astype(BF), gain, shift)
+        else:
+            normed_rows = gather_tokens(normed.astype(BF))
+        if layer:
+            weights.append(tuple(placed(*pair, normed_rows) for pair in zip(lines, others)))
         qkv_full, up_full, fall_full = weights[layer]
-        normed, unit, scale_inv = layer_norm(current, gains[layer][None], shifts[layer][None])
-        normed_rows = gather_tokens(normed.astype(BF))
         query, own, tail = qkv_call(normed_rows, qkv_full, joint_bias[layer], tables)
         near = lax.ppermute(own, "seq", shifted(seq_count, 1))
         far = lax.ppermute(tail, "seq", shifted(seq_count, 2))
+        if layer + 1 < layers:
+            held, _ = lax.optimization_barrier((pieces[layer + 1], (near, far)))
+            lines = [gather_line(piece) for piece in held]
+            others = [other_sides(line) for line in lines]
         hidden, slope = up_call(normed_rows, up_full, rise_bias[layer])
         mixed, lse = fwd_call(counts, query, own, near, far)
+        if GATES and layer + 1 < layers:
+            mixed, _ = lax.optimization_barrier((mixed, lines[0][1:]))
         partial = dot_nt(mixed, fall_full[:, :head_width]) + dot_nt(hidden, fall_full[:, head_width:])
         branch = scatter_tokens(partial.astype(BF))
+        if GATES and layer + 1 < layers:
+            branch, _ = lax.optimization_barrier((branch, others[0]))
         kept.append((normed_rows, unit, scale_inv, query, own, near, far, hidden, slope, mixed, lse))
         current = current + branch + out_biases[layer][None, :]
 
@@ -732,7 +811,7 @@
     )
 
 
-GATHER = (gather_rows, gather_rows_whole)
+GATES = True
 WHOLE = (False, True)
 
 

time: 732 us -> 717 us (0.980)
  waiting for transfers between devices: 315 us -> 201 us
  starting transfers between devices: 117 us -> 198 us
  Pallas kernels: 122 us -> 147 us
  local copies, waits for them, and re-layouts: 63.6 us -> 48.8 us
    ppermute x12 -> x42, starting transfers between devices: 18.7 us -> 106 us  [the longest x18 61.7 us: gather_line(): lax.ppermute(piece, 'seq', rolled_outer(outer, distance))]
    all_to_all x2, waiting for transfers between devices: 39.5 us -> 4.97 us  [exchanged(): return lax.all_to_all(rows, ('seq', 'tensor'), 0, 0, tiled=True)]
    pallas_call x0 -> x7, Pallas kernels: none -> 28.5 us  [the longest x6 24.8 us: place_sides_call(): pl.pallas_call(place_sides_kernel, grid_spec=pltpu.PrefetchScalarGridSpec...]
    ppermute x4, waiting for transfers between devices: 41 us -> 13.1 us  [gather_tokens(): across = lax.ppermute(rows, 'tensor', flipped(count, 2))]
    ppermute x12 -> x42, waiting for transfers between devices: 61.7 us -> 37.4 us  [the longest x18 21.7 us: gather_line(): lax.ppermute(piece, 'seq', rolled_outer(outer, distance))]
    dynamic_update_slice x16 -> x0, local copies, waits for them, and re-layouts: 18.7 us -> none  [the longest x9 8.39 us: gather_rows(): lax.dynamic_update_index_in_dim(line, came, (at - distance) % outer, 0)]
    ppermute x2, waiting for transfers between devices: 17.8 us -> 0.01 us  [local(): near = lax.ppermute(own, 'seq', shifted(seq_count, 1))]
    ppermute x2, starting transfers between devices: 10.4 us -> 28 us  [local(): far = lax.ppermute(tail, 'seq', shifted(seq_count, 2))]
  transfers between devices with their start and end apart: 58 -> 85, of which waited for: 26 -> 25; matrix products, arithmetic and copies ran while one was open for 18% -> 16% of each run, Pallas kernels for 13% -> 17%
where the time goes in v3:
time: 717 us; the launch traced here: 711 us
  waiting for transfers between devices  201 us (28%)
  starting transfers between devices  198 us (28%)
  Pallas kernels  147 us (21%)
  matrix products  58.6 us (8%)
  local copies, waits for them, and re-layouts  48.8 us (7%)
  other arithmetic  41.7 us (6%)
  between operations  16 us (2%)
    ppermute x2, waiting for transfers between devices, local(): came_far = lax.ppermute(dfar, 'seq', shifted(seq_count, -2))  86.5 us
    ppermute x18, starting transfers between devices, gather_line(): lax.ppermute(piece, 'seq', rolled_outer(outer, distance))  61.7 us
    ppermute x24, starting transfers between devices, other_sides(): return [lax.ppermute(shard, 'seq', flipped(count, 1)) for shard in line]  44.2 us
    ppermute x9, starting transfers between devices, scatter_grad(): lax.ppermute(part, 'seq', rolled_outer(outer, distance)).astype(F32)  34.6 us
    ppermute x2, starting transfers between devices, local(): far = lax.ppermute(tail, 'seq', shifted(seq_count, 2))  28 us
    ppermute x9, waiting for transfers between devices, scatter_grad(): lax.ppermute(part, 'seq', rolled_outer(outer, distance)).astype(F32)  27.6 us
    ppermute x4, waiting for transfers between devices, scatter_tokens(): across = lax.ppermute(far.astype(BF), 'tensor', flipped(count, 2))  26.3 us
    pallas_call x6, Pallas kernels, place_sides_call(): pl.pallas_call(place_sides_kernel, grid_spec=pltpu.PrefetchScalarGridSpec...  24.8 us
  transfers between devices with their start and end apart: 85, of which 25 were waited for; matrix products, arithmetic and copies ran while one was open for 16% of the time, Pallas kernels for 17%

profile of v3, /device:TPU:0, one launch (start us, length us, event | category | flops | bytes accessed | tf_op | source)
XLA Modules:
  0.0 710.6 jit_solution(7296186138290571260)
XLA Ops:
  98.6 17.1 %collective-permute-start.11 = (bf16[2,512,256]{2,1,0:T(8,128)(2,1)}, bf16[2,512,256]{2,1,0:T(8,128)(2,1)S(1)}, u32[]{:S(2)}, u32[]{:S(2)}) collective-permute-start(bf16[2,512,256]{2,1,0:T(8,128)(2,1)} %get-tuple-element.65), channel_id=1, source_target_pairs={{0,8},{4,12},{8,16},{12,20},{16,24},{20,28},{1,9},{5,13},{9,17},{1... | collective-permute-start | bytes 1572872 | tf_op jit(solution)/shard_map/ppermute | solution.py:710
  115.7 8.3 %collective-permute-start.22 = (bf16[128,1280]{1,0:T(8,128)(2,1)}, bf16[128,1280]{1,0:T(8,128)(2,1)}, u32[]{:S(2)}, u32[]{:S(2)}) collective-permute-start(bf16[128,1280]{1,0:T(8,128)(2,1)} %collective-permute-done.18.refs_1_), channel_id=1, source_target_pairs={{0,4},{4,0},{8,12},{12,8},{16,20},{20,16},{24,28},{28,24},{1,5},{5... | collective-permute-start | bytes 983048 | tf_op jit(solution)/shard_map/ppermute | solution.py:529
  124.0 7.1 collective-permute-start.23
  136.5 7.8 %up.2 = (bf16[1024,1024]{1,0:T(8,128)(2,1)}, f32[1024,1024]{1,0:T(8,128)}) custom-call(bf16[1024,1024]{1,0:T(8,128)(2,1)} %place_norm.1.x_ref.left_ref, bf16[1024,1024]{1,0:T(8,128)(2,1)} %bitcast.157, f32[1,1024]{1,0:T(1,128)} %squeeze.75.b_ref), custom_call_target="tpu_custom_call" | custom-call | tf_op jit(solution)/shard_map/up/pallas_call | solution.py:336
  149.0 12.8 %collective-permute-start.12 = (bf16[128,768]{1,0:T(8,128)(2,1)S(1)}, bf16[128,768]{1,0:T(8,128)(2,1)S(1)}, u32[]{:S(2)}, u32[]{:S(2)}) collective-permute-start(bf16[128,768]{1,0:T(8,128)(2,1)S(1)} %copy.112.refs_0_), channel_id=1, source_target_pairs={{0,8},{4,12},{8,16},{12,20},{16,24},{20,28},{24,0},{28,4},{1,9},{5... | collective-permute-start | bytes 589832 | tf_op jit(solution)/shard_map/ppermute | solution.py:523
  172.1 7.8 %attend.2 = (bf16[1024,256]{1,0:T(8,128)(2,1)}, f32[2,2,1024]{2,1,0:T(2,128)}) custom-call(s32[2]{0:T(128)} %fusion.28.n_ref, bf16[1024,256]{1,0:T(8,128)(2,1)} %get-tuple-element.63.q_ref, bf16[2,2,512,256]{3,2,1,0:T(8,128)(2,1)} %get-tuple-element.64.own_ref, bf16[2,2,512,256]{3,2,1,0:T(8,128)(2,1)} %copy-done.4, bf16[2,512,256]{2,1,0:T(8,128)(2,1)} %copy-done.21), custom_call_target="tpu_custom_call" | custom-call | tf_op jit(solution)/shard_map/attend/pallas_call | solution.py:161
  210.2 6.9 collective-permute-start.48
  242.4 12.9 %collective-permute-done.41.refs_2_ = bf16[128,1280]{1,0:T(8,128)(2,1)} collective-permute-done((bf16[128,1280]{1,0:T(8,128)(2,1)S(1)}, bf16[128,1280]{1,0:T(8,128)(2,1)}, u32[]{:S(2)}, u32[]{:S(2)}) %collective-permute-start.41) | collective-permute-done | bytes 327712 | tf_op jit(solution)/shard_map/ppermute | solution.py:523
  297.6 7.7 %up.3 = (bf16[1024,1024]{1,0:T(8,128)(2,1)}, f32[1024,1024]{1,0:T(8,128)}) custom-call(bf16[1024,1024]{1,0:T(8,128)(2,1)} %place.3.x_ref, bf16[1024,1024]{1,0:T(8,128)(2,1)} %bitcast.159, f32[1,1024]{1,0:T(1,128)} %squeeze.78.b_ref), custom_call_target="tpu_custom_call" | custom-call | tf_op jit(solution)/shard_map/up/pallas_call | solution.py:336
  308.7 10.9 %collective-permute-start.39 = (bf16[2,512,256]{2,1,0:T(8,128)(2,1)}, bf16[2,512,256]{2,1,0:T(8,128)(2,1)}, u32[]{:S(2)}, u32[]{:S(2)}) collective-permute-start(bf16[2,512,256]{2,1,0:T(8,128)(2,1)} %get-tuple-element.76), channel_id=1, source_target_pairs={{0,8},{4,12},{8,16},{12,20},{16,24},{20,28},{1,9},{5,13},{9,17},{1... | collective-permute-start | bytes 1572872 | tf_op jit(solution)/shard_map/ppermute | solution.py:710
  334.2 7.7 %attend.3 = (bf16[1024,256]{1,0:T(8,128)(2,1)}, f32[2,2,1024]{2,1,0:T(2,128)}) custom-call(s32[2]{0:T(128)} %fusion.28.n_ref, bf16[1024,256]{1,0:T(8,128)(2,1)} %get-tuple-element.74.q_ref, bf16[2,2,512,256]{3,2,1,0:T(8,128)(2,1)} %get-tuple-element.75.own_ref, bf16[2,2,512,256]{3,2,1,0:T(8,128)(2,1)} %copy-done.5, ...), custom_call_target="tpu_custom_call" | custom-call | tf_op jit(solution)/shard_map/attend/pallas_call | solution.py:161
  342.0 12.3 %attend_back.2 = (bf16[1024,256]{1,0:T(8,128)(2,1)}, f32[2,2,512,256]{3,2,1,0:T(8,128)}, bf16[2,2,512,256]{3,2,1,0:T(8,128)(2,1)}, bf16[2,512,256]{2,1,0:T(8,128)(2,1)}) custom-call(s32[2]{0:T(128)} %fusion.28.n_ref, bf16[1024,256]{1,0:T(8,128)(2,1)} %get-tuple-element.74.q_ref, bf16[2,2,512,256]{3,2,1,0:T(8,128)(2,1)} %get-tuple-element.75.own_ref, ...), custom_call_target="tpu_custom_call" | custom-call | tf_op jit(solution)/shard_map/attend_back/pallas_call | solution.py:244
  367.2 37.0 %collective-permute-done.60.far_ref = bf16[2,512,256]{2,1,0:T(8,128)(2,1)S(1)} collective-permute-done((bf16[2,512,256]{2,1,0:T(8,128)(2,1)S(1)}, bf16[2,512,256]{2,1,0:T(8,128)(2,1)S(1)}, u32[]{:S(2)}, u32[]{:S(2)}) %collective-permute-start.60) | collective-permute-done | bytes 524320 | tf_op jit(solution)/shard_map/ppermute | solution.py:739
  436.6 11.2 %collective-permute-done.62 = bf16[256,1024]{1,0:T(8,128)(2,1)} collective-permute-done((bf16[256,1024]{1,0:T(8,128)(2,1)}, bf16[256,1024]{1,0:T(8,128)(2,1)}, u32[]{:S(2)}, u32[]{:S(2)}) %collective-permute-start.62) | collective-permute-done | bytes 524320 | tf_op jit(solution)/shard_map/ppermute | solution.py:577
  449.9 8.6 %collective-permute-done.55 = bf16[256,1024]{1,0:T(8,128)(2,1)S(1)} collective-permute-done((bf16[256,1024]{1,0:T(8,128)(2,1)S(1)}, bf16[256,1024]{1,0:T(8,128)(2,1)S(1)}, u32[]{:S(2)}, u32[]{:S(2)}) %collective-permute-start.55) | collective-permute-done | bytes 524320 | tf_op jit(solution)/shard_map/ppermute | solution.py:577
  461.9 13.1 %collective-permute-done.64.across_ref = bf16[256,1024]{1,0:T(8,128)(2,1)S(1)} collective-permute-done((bf16[256,1024]{1,0:T(8,128)(2,1)S(1)}, bf16[256,1024]{1,0:T(8,128)(2,1)S(1)}, u32[]{:S(2)}, u32[]{:S(2)}) %collective-permute-start.64) | collective-permute-done | bytes 524320 | tf_op jit(solution)/shard_map/ppermute | solution.py:559
  483.7 12.2 %attend_back.3 = (bf16[1024,256]{1,0:T(8,128)(2,1)}, f32[2,2,512,256]{3,2,1,0:T(8,128)}, bf16[2,2,512,256]{3,2,1,0:T(8,128)(2,1)}, bf16[2,512,256]{2,1,0:T(8,128)(2,1)}) custom-call(s32[2]{0:T(128)} %fusion.28.n_ref, bf16[1024,256]{1,0:T(8,128)(2,1)} %get-tuple-element.63.q_ref, bf16[2,2,512,256]{3,2,1,0:T(8,128)(2,1)} %get-tuple-element.64.own_ref, ...), custom_call_target="tpu_custom_call" | custom-call | tf_op jit(solution)/shard_map/attend_back/pallas_call | solution.py:244
  499.6 6.9 weight_grad.4
  510.5 7.3 %convert_reduce_fusion.1 = (f32[1024]{0:T(1024)S(1)}, bf16[1024,1024]{1,0:T(8,128)(2,1)}) fusion(f32[1024,1024]{1,0:T(8,128)} %get-tuple-element.88, bf16[1024,1024]{1,0:T(8,128)(2,1)} %place.5.left_ref, bf16[1024,1280]{1,0:T(8,128)(2,1)} %bitcast.168), kind=kOutput, calls=%fused_computation.2 | convolution fusion | flops 2151676928 | bytes 10489856 | tf_op jit(solution)/shard_map/dot_general | solution.py:21
  524.2 49.4 %collective-permute-done.67.far_ref = bf16[2,512,256]{2,1,0:T(8,128)(2,1)} collective-permute-done((bf16[2,512,256]{2,1,0:T(8,128)(2,1)}, bf16[2,512,256]{2,1,0:T(8,128)(2,1)}, u32[]{:S(2)}, u32[]{:S(2)}) %collective-permute-start.67) | collective-permute-done | bytes 524320 | tf_op jit(solution)/shard_map/ppermute | solution.py:739
  597.8 10.3 %collective-permute-start.81 = (bf16[128,1024]{1,0:T(8,128)(2,1)}, bf16[128,1024]{1,0:T(8,128)(2,1)}, u32[]{:S(2)}, u32[]{:S(2)}) collective-permute-start(bf16[128,1024]{1,0:T(8,128)(2,1)} %get-tuple-element.114), channel_id=1, source_target_pairs={{0,24},{4,28},{8,0},{12,4},{16,8},{20,12},{24,16},{28,20},{1,25},{... | collective-permute-start | bytes 786440 | tf_op jit(solution)/shard_map/ppermute | solution.py:552
  619.5 12.4 %collective-permute-done.80 = bf16[128,1024]{1,0:T(8,128)(2,1)} collective-permute-done((bf16[128,1024]{1,0:T(8,128)(2,1)}, bf16[128,1024]{1,0:T(8,128)(2,1)}, u32[]{:S(2)}, u32[]{:S(2)}) %collective-permute-start.80) | collective-permute-done | bytes 262176 | tf_op jit(solution)/shard_map/ppermute | solution.py:552
  631.9 14.6 %collective-permute-start.75 = (bf16[128,1280]{1,0:T(8,128)(2,1)}, bf16[128,1280]{1,0:T(8,128)(2,1)}, u32[]{:S(2)}, u32[]{:S(2)}) collective-permute-start(bf16[128,1280]{1,0:T(8,128)(2,1)} %get-tuple-element.106), channel_id=1, source_target_pairs={{0,8},{4,12},{8,16},{12,20},{16,24},{20,28},{24,0},{28,4},{1,9},{5... | collective-permute-start | bytes 983048 | tf_op jit(solution)/shard_map/ppermute | solution.py:552
  658.3 10.0 %collective-permute-done.76 = bf16[128,1280]{1,0:T(8,128)(2,1)} collective-permute-done((bf16[128,1280]{1,0:T(8,128)(2,1)}, bf16[128,1280]{1,0:T(8,128)(2,1)}, u32[]{:S(2)}, u32[]{:S(2)}) %collective-permute-start.76) | collective-permute-done | bytes 327712 | tf_op jit(solution)/shard_map/ppermute | solution.py:552
  (522 shorter events, 382.3 us)
Async XLA Ops:
  26.5 671.1 %reduce-scatter.2.cloned.1.call-start = ((), (), s32[]{:S(2)}) async-start(), calls=%async_computation.3 | async-start | bytes 7077888 | tf_op jit(solution)/shard_map/reduce_scatter | solution.py:756
  79.3 69.5 %collective-permute-start.10 = (bf16[2,2,512,256]{3,2,1,0:T(8,128)(2,1)}, bf16[2,2,512,256]{3,2,1,0:T(8,128)(2,1)S(1)}, u32[]{:S(2)}, u32[]{:S(2)}) collective-permute-start(bf16[2,2,512,256]{3,2,1,0:T(8,128)(2,1)} %get-tuple-element.64.own_ref), channel_id=1, source_target_pairs={{0,4},{4,8},{8,12},{12,16},{16,20},{20,24},{24,28},{1,5},{5,9},{9,... | collective-permute-start | bytes 3145736 | tf_op jit(solution)/shard_map/ppermute | solution.py:709
  92.3 31.6 %collective-permute-start.20 = (bf16[128,1280]{1,0:T(8,128)(2,1)S(1)}, bf16[128,1280]{1,0:T(8,128)(2,1)}, u32[]{:S(2)}, u32[]{:S(2)}) collective-permute-start(bf16[128,1280]{1,0:T(8,128)(2,1)S(1)} %pad_maximum_fusion.5.refs_0_), channel_id=1, source_target_pairs={{0,24},{4,28},{8,0},{12,4},{16,8},{20,12},{24,16},{28,20},{1,25},{... | collective-permute-start | bytes 983048 | tf_op jit(solution)/shard_map/ppermute | solution.py:523
  92.5 38.5 %collective-permute-start.21 = (bf16[128,1280]{1,0:T(8,128)(2,1)S(1)}, bf16[128,1280]{1,0:T(8,128)(2,1)}, u32[]{:S(2)}, u32[]{:S(2)}) collective-permute-start(bf16[128,1280]{1,0:T(8,128)(2,1)S(1)} %pad_maximum_fusion.5.refs_0_), channel_id=1, source_target_pairs={{0,4},{4,0},{8,12},{12,8},{16,20},{20,16},{24,28},{28,24},{1,5},{5... | collective-permute-start | bytes 983048 | tf_op jit(solution)/shard_map/ppermute | solution.py:529
  98.6 50.2 %collective-permute-start.11 = (bf16[2,512,256]{2,1,0:T(8,128)(2,1)}, bf16[2,512,256]{2,1,0:T(8,128)(2,1)S(1)}, u32[]{:S(2)}, u32[]{:S(2)}) collective-permute-start(bf16[2,512,256]{2,1,0:T(8,128)(2,1)} %get-tuple-element.65), channel_id=1, source_target_pairs={{0,8},{4,12},{8,16},{12,20},{16,24},{20,28},{1,9},{5,13},{9,17},{1... | collective-permute-start | bytes 1572872 | tf_op jit(solution)/shard_map/ppermute | solution.py:710
  149.0 30.9 %collective-permute-start.12 = (bf16[128,768]{1,0:T(8,128)(2,1)S(1)}, bf16[128,768]{1,0:T(8,128)(2,1)S(1)}, u32[]{:S(2)}, u32[]{:S(2)}) collective-permute-start(bf16[128,768]{1,0:T(8,128)(2,1)S(1)} %copy.112.refs_0_), channel_id=1, source_target_pairs={{0,8},{4,12},{8,16},{12,20},{16,24},{20,28},{24,0},{28,4},{1,9},{5... | collective-permute-start | bytes 589832 | tf_op jit(solution)/shard_map/ppermute | solution.py:523
  225.8 33.2 %collective-permute-start.36 = (bf16[256,1024]{1,0:T(8,128)(2,1)S(1)}, bf16[256,1024]{1,0:T(8,128)(2,1)S(1)}, u32[]{:S(2)}, u32[]{:S(2)}) collective-permute-start(bf16[256,1024]{1,0:T(8,128)(2,1)S(1)} %add_convert_fusion.4.own_ref), channel_id=1, source_target_pairs={{0,2},{1,3},{2,0},{3,1},{4,6},{5,7},{6,4},{7,5},{8,10},{9,11},{10,... | collective-permute-start | bytes 1572872 | tf_op jit(solution)/shard_map/ppermute | solution.py:559
  259.0 30.9 %collective-permute-start.58 = (bf16[256,1024]{1,0:T(8,128)(2,1)S(1)}, bf16[256,1024]{1,0:T(8,128)(2,1)}, u32[]{:S(2)}, u32[]{:S(2)}) collective-permute-start(bf16[256,1024]{1,0:T(8,128)(2,1)S(1)} %collective-permute-done.57.across_ref), channel_id=1, source_target_pairs={{0,1},{1,0},{2,3},{3,2},{4,5},{5,4},{6,7},{7,6},{8,9},{9,8},{10,11... | collective-permute-start | bytes 1572872 | tf_op jit(solution)/shard_map/ppermute | solution.py:561
  270.0 38.7 %collective-permute-start.43 = (bf16[128,1280]{1,0:T(8,128)(2,1)S(1)}, bf16[128,1280]{1,0:T(8,128)(2,1)}, u32[]{:S(2)}, u32[]{:S(2)}) collective-permute-start(bf16[128,1280]{1,0:T(8,128)(2,1)S(1)} %pad_maximum_fusion.4.refs_0_), channel_id=1, source_target_pairs={{0,4},{4,0},{8,12},{12,8},{16,20},{20,16},{24,28},{28,24},{1,5},{5... | collective-permute-start | bytes 983048 | tf_op jit(solution)/shard_map/ppermute | solution.py:529
  270.3 49.3 %collective-permute-start.44 = (bf16[128,1280]{1,0:T(8,128)(2,1)}, bf16[128,1280]{1,0:T(8,128)(2,1)}, u32[]{:S(2)}, u32[]{:S(2)}) collective-permute-start(bf16[128,1280]{1,0:T(8,128)(2,1)} %collective-permute-done.40.refs_1_), channel_id=1, source_target_pairs={{0,4},{4,0},{8,12},{12,8},{16,20},{20,16},{24,28},{28,24},{1,5},{5... | collective-permute-start | bytes 983048 | tf_op jit(solution)/shard_map/ppermute | solution.py:529
  272.9 46.7 %collective-permute-start.45 = (bf16[128,1280]{1,0:T(8,128)(2,1)}, bf16[128,1280]{1,0:T(8,128)(2,1)}, u32[]{:S(2)}, u32[]{:S(2)}) collective-permute-start(bf16[128,1280]{1,0:T(8,128)(2,1)} %collective-permute-done.41.refs_2_), channel_id=1, source_target_pairs={{0,4},{4,0},{8,12},{12,8},{16,20},{20,16},{24,28},{28,24},{1,5},{5... | collective-permute-start | bytes 983048 | tf_op jit(solution)/shard_map/ppermute | solution.py:529
  273.2 46.4 %collective-permute-start.46 = (bf16[128,1280]{1,0:T(8,128)(2,1)}, bf16[128,1280]{1,0:T(8,128)(2,1)}, u32[]{:S(2)}, u32[]{:S(2)}) collective-permute-start(bf16[128,1280]{1,0:T(8,128)(2,1)} %collective-permute-done.42.refs_3_), channel_id=1, source_target_pairs={{0,4},{4,0},{8,12},{12,8},{16,20},{20,16},{24,28},{28,24},{1,5},{5... | collective-permute-start | bytes 983048 | tf_op jit(solution)/shard_map/ppermute | solution.py:529
  289.9 43.4 %collective-permute-start.38 = (bf16[2,2,512,256]{3,2,1,0:T(8,128)(2,1)}, bf16[2,2,512,256]{3,2,1,0:T(8,128)(2,1)S(1)}, u32[]{:S(2)}, u32[]{:S(2)}) collective-permute-start(bf16[2,2,512,256]{3,2,1,0:T(8,128)(2,1)} %get-tuple-element.75.own_ref), channel_id=1, source_target_pairs={{0,4},{4,8},{8,12},{12,16},{16,20},{20,24},{24,28},{1,5},{5,9},{9,... | collective-permute-start | bytes 3145736 | tf_op jit(solution)/shard_map/ppermute | solution.py:709
  354.3 50.0 %collective-permute-start.59 = (bf16[2,2,512,256]{3,2,1,0:T(8,128)(2,1)}, bf16[2,2,512,256]{3,2,1,0:T(8,128)(2,1)}, u32[]{:S(2)}, u32[]{:S(2)}) collective-permute-start(bf16[2,2,512,256]{3,2,1,0:T(8,128)(2,1)} %get-tuple-element.85), channel_id=1, source_target_pairs={{4,0},{8,4},{12,8},{16,12},{20,16},{24,20},{28,24},{5,1},{9,5},{13... | collective-permute-start | bytes 3145736 | tf_op jit(solution)/shard_map/ppermute | solution.py:738
  361.7 42.6 %collective-permute-start.60 = (bf16[2,512,256]{2,1,0:T(8,128)(2,1)S(1)}, bf16[2,512,256]{2,1,0:T(8,128)(2,1)S(1)}, u32[]{:S(2)}, u32[]{:S(2)}) collective-permute-start(bf16[2,512,256]{2,1,0:T(8,128)(2,1)S(1)} %copy-done.88), channel_id=1, source_target_pairs={{8,0},{12,4},{16,8},{20,12},{24,16},{28,20},{9,1},{13,5},{17,9},{2... | collective-permute-start | bytes 1572872 | tf_op jit(solution)/shard_map/ppermute | solution.py:739
  495.9 77.8 %collective-permute-start.66 = (bf16[2,2,512,256]{3,2,1,0:T(8,128)(2,1)}, bf16[2,2,512,256]{3,2,1,0:T(8,128)(2,1)S(1)}, u32[]{:S(2)}, u32[]{:S(2)}) collective-permute-start(bf16[2,2,512,256]{3,2,1,0:T(8,128)(2,1)} %get-tuple-element.92), channel_id=1, source_target_pairs={{4,0},{8,4},{12,8},{16,12},{20,16},{24,20},{28,24},{5,1},{9,5},{13... | collective-permute-start | bytes 3145736 | tf_op jit(solution)/shard_map/ppermute | solution.py:738
  506.5 67.2 %collective-permute-start.67 = (bf16[2,512,256]{2,1,0:T(8,128)(2,1)}, bf16[2,512,256]{2,1,0:T(8,128)(2,1)}, u32[]{:S(2)}, u32[]{:S(2)}) collective-permute-start(bf16[2,512,256]{2,1,0:T(8,128)(2,1)} %get-tuple-element.93), channel_id=1, source_target_pairs={{8,0},{12,4},{16,8},{20,12},{24,16},{28,20},{9,1},{13,5},{17,9},{2... | collective-permute-start | bytes 1572872 | tf_op jit(solution)/shard_map/ppermute | solution.py:739
  507.7 100.4 %collective-permute-start.74 = (bf16[4,128,1280]{2,1,0:T(8,128)(2,1)}, bf16[4,128,1280]{2,1,0:T(8,128)(2,1)}, u32[]{:S(2)}, u32[]{:S(2)}) collective-permute-start(bf16[4,128,1280]{2,1,0:T(8,128)(2,1)} %get-tuple-element.104), channel_id=1, source_target_pairs={{0,4},{4,0},{8,12},{12,8},{16,20},{20,16},{24,28},{28,24},{1,5},{5... | collective-permute-start | bytes 3932168 | tf_op jit(solution)/shard_map/ppermute | solution.py:549
  524.1 70.1 %collective-permute-start.78 = (bf16[4,128,1024]{2,1,0:T(8,128)(2,1)}, bf16[4,128,1024]{2,1,0:T(8,128)(2,1)}, u32[]{:S(2)}, u32[]{:S(2)}) collective-permute-start(bf16[4,128,1024]{2,1,0:T(8,128)(2,1)} %get-tuple-element.110), channel_id=1, source_target_pairs={{0,4},{4,0},{8,12},{12,8},{16,20},{20,16},{24,28},{28,24},{1,5},{5... | collective-permute-start | bytes 3145736 | tf_op jit(solution)/shard_map/ppermute | solution.py:549
  587.6 64.6 %collective-permute-start.68 = (bf16[2,256,1024]{2,1,0:T(8,128)(2,1)S(1)}, bf16[2,256,1024]{2,1,0:T(8,128)(2,1)}, u32[]{:S(2)}, u32[]{:S(2)}) collective-permute-start(bf16[2,256,1024]{2,1,0:T(8,128)(2,1)S(1)} %dynamic-slice_bitcast_fusion), channel_id=1, source_target_pairs={{0,1},{1,0},{2,3},{3,2},{4,5},{5,4},{6,7},{7,6},{8,9},{9,8},{10,11... | collective-permute-start | bytes 3145736 | tf_op jit(solution)/shard_map/ppermute | solution.py:574
  593.5 55.2 %collective-permute-start.70 = (bf16[4,128,768]{2,1,0:T(8,128)(2,1)}, bf16[4,128,768]{2,1,0:T(8,128)(2,1)}, u32[]{:S(2)}, u32[]{:S(2)}) collective-permute-start(bf16[4,128,768]{2,1,0:T(8,128)(2,1)} %get-tuple-element.98), channel_id=1, source_target_pairs={{0,4},{4,0},{8,12},{12,8},{16,20},{20,16},{24,28},{28,24},{1,5},{5... | collective-permute-start | bytes 2359304 | tf_op jit(solution)/shard_map/ppermute | solution.py:549
  615.1 43.1 %collective-permute-start.77 = (bf16[128,1280]{1,0:T(8,128)(2,1)}, bf16[128,1280]{1,0:T(8,128)(2,1)S(1)}, u32[]{:S(2)}, u32[]{:S(2)}) collective-permute-start(bf16[128,1280]{1,0:T(8,128)(2,1)} %get-tuple-element.108), channel_id=1, source_target_pairs={{0,24},{4,28},{8,0},{12,4},{16,8},{20,12},{24,16},{28,20},{1,25},{... | collective-permute-start | bytes 983048 | tf_op jit(solution)/shard_map/ppermute | solution.py:552
  631.9 36.4 %collective-permute-start.76 = (bf16[128,1280]{1,0:T(8,128)(2,1)}, bf16[128,1280]{1,0:T(8,128)(2,1)}, u32[]{:S(2)}, u32[]{:S(2)}) collective-permute-start(bf16[128,1280]{1,0:T(8,128)(2,1)} %get-tuple-element.107), channel_id=1, source_target_pairs={{0,16},{4,20},{8,24},{12,28},{16,0},{20,4},{24,8},{28,12},{1,17},{... | collective-permute-start | bytes 983048 | tf_op jit(solution)/shard_map/ppermute | solution.py:552
  631.9 37.8 %collective-permute-start.75 = (bf16[128,1280]{1,0:T(8,128)(2,1)}, bf16[128,1280]{1,0:T(8,128)(2,1)}, u32[]{:S(2)}, u32[]{:S(2)}) collective-permute-start(bf16[128,1280]{1,0:T(8,128)(2,1)} %get-tuple-element.106), channel_id=1, source_target_pairs={{0,8},{4,12},{8,16},{12,20},{16,24},{20,28},{24,0},{28,4},{1,9},{5... | collective-permute-start | bytes 983048 | tf_op jit(solution)/shard_map/ppermute | solution.py:552
  (151 other events, 2475.1 us)
Sparse Core Ops, SparseCore 0:
  417.8 142.8 reduce-scatter.1
